TPU v7x, 32 devices: a whole 2x2x4 slice. The times are simulated.
32 devices in a mesh: section: 2 (over y), replica: 16 (over z, x, core).
Axes of the slice: x: 2, y: 2, z: 4, core: 2. Of those that a mesh axis runs over, the one named last changes fastest.
Arguments:
- coords_in: bfloat16 [2, 2048, 512], P(None, 'replica'), may hold values from -6 to 6
- token_rows: bfloat16 [2, 2048, 2048], P(None, 'replica'), may hold values from -6 to 6
- cotangent: bfloat16 [2, 2048, 512], P(None, 'replica'), may hold values from -6 to 6
- subspace_basis: bfloat16 [512, 2048], replicated, may hold values from -0.25 to 0.25
- norm_gain: float32 [2, 2048], P('section'), may hold values from 0.5 to 1.5
- gate_weight: float32 [2, 2048, 256], P('section', 'replica'), may hold values from -0.125 to 0.125
- up_weight: bfloat16 [2, 2048, 256], P('section', 'replica'), may hold values from -0.125 to 0.125
- down_weight: float32 [2, 256, 512], P('section', 'replica'), may hold values from -0.375 to 0.375
- gate_moment: float32 [2, 2048, 256], P('section', 'replica'), may hold values from -0.625 to 0.625
- gate_second: float32 [2, 2048, 256], P('section', 'replica'), may hold values from 0.01 to 0.1
- down_moment: float32 [2, 256, 512], P('section', 'replica'), may hold values from -0.625 to 0.625
- down_second: float32 [2, 256, 512], P('section', 'replica'), may hold values from 0.01 to 0.1
Outputs:
- section_coords: bfloat16 [2, 2, 2048, 512], P('section', None, 'replica')
- coord_grads: bfloat16 [2, 2, 2048, 512], P('section', None, 'replica')
- gate_new: float32 [2, 2048, 256], P('section', 'replica')
- gate_moment_new: float32 [2, 2048, 256], P('section', 'replica')
- gate_second_new: float32 [2, 2048, 256], P('section', 'replica')
- down_new: float32 [2, 256, 512], P('section', 'replica')
- down_moment_new: float32 [2, 256, 512], P('section', 'replica')
- down_second_new: float32 [2, 256, 512], P('section', 'replica')
All inputs are finite; a program needn't handle non-finite values.
Results may differ from a plain program's by a relative error of at most 0.03.
Values may be sent and summed in bfloat16 or wider, within the bound.
No kernel may reach another device: no remote copies, remote signals or barrier semaphores. Data moves between devices by JAX's collectives and lax.ppermute only.
A program may use at most 64 MiB of HBM per device.

v0:
```python
import functools
import math

import jax
import jax.numpy as jnp
from jax import lax
from jax.experimental import pallas as pl
from jax.experimental.pallas import tpu as pltpu
from jax.sharding import PartitionSpec as P


epsilon = 1e-06
learn_rate = 0.001
decay_first = 0.9
decay_second = 0.95
step_count = 10
adam_floor = 1e-08


def contract_last(left, right):
    return lax.dot_general(
        left, right, (((1,), (1,)), ((), ())), preferred_element_type=jnp.float32
    )


def contract_first(left, right):
    return lax.dot_general(
        left, right, (((0,), (0,)), ((), ())), preferred_element_type=jnp.float32
    )


def shift(value, axis, steps):
    count = lax.axis_size(axis)
    first, last = max(0, -steps), min(count, count - steps)
    return lax.ppermute(value, axis, [(source, source + steps) for source in range(first, last)])


def bit_orders(replicas, kinds="ab"):
    bits = (replicas // 2).bit_length() - 1
    down = list(range(bits - 1, -1, -1))
    known = {"a": down, "b": down[-1:] + down[:-1], "c": down[:1] + down[-1:] + down[1:-1], "d": down[1:-1] + down[:1] + down[-1:]}
    return [known[kind] if bits > 1 else down for kind in kinds]


def exchange(value, replicas, turn, kinds="ab"):
    orders = bit_orders(replicas, kinds)
    pairs = [(r, r ^ (2 << orders[r % 2][turn])) for r in range(replicas)]
    return lax.ppermute(value, "replica", pairs)


def swap_sections(value):
    return lax.ppermute(value, "section", [(0, 1), (1, 0)])


def swap_cores(value, replicas):
    return lax.ppermute(value, "replica", [(r, r ^ 1) for r in range(replicas)])


def offsets(replicas, kinds="ab"):
    tables = []
    for order in bit_orders(replicas, kinds):
        places = [0]
        for bit in order:
            places = places + [place ^ (1 << bit) for place in places]
        tables.append(places)
    return tables


def chip_at(replica, core, table, place):
    return (replica // 2) ^ jnp.where(core == 0, table[0][place], table[1][place])


def gather_shares(share):
    replicas = lax.axis_size("replica")
    replica = lax.axis_index("replica")
    core = replica % 2
    table = offsets(replicas)
    held = share[None]
    for turn in range(len(table[0]).bit_length() - 1):
        held = jnp.concatenate([held, exchange(held, replicas, turn)], axis=0)
    other = swap_cores(held, replicas)
    result = jnp.zeros((replicas,) + share.shape, share.dtype)
    for place in range(replicas // 2):
        mine = chip_at(replica, core, table, place) * 2 + core
        theirs = chip_at(replica, 1 - core, table, place) * 2 + 1 - core
        result = lax.dynamic_update_slice(result, held[place][None], (mine, 0, 0))
        result = lax.dynamic_update_slice(result, other[place][None], (theirs, 0, 0))
    return result


def reduce_shares(partial):
    replicas = lax.axis_size("replica")
    replica = lax.axis_index("replica")
    core = replica % 2
    table = offsets(replicas)
    halves = partial.reshape((replicas // 2, 2) + partial.shape[1:])
    sent = jnp.where(core == 0, halves[:, 1], halves[:, 0])
    kept = jnp.where(core == 0, halves[:, 0], halves[:, 1])
    total = kept.astype(jnp.float32) + swap_cores(sent, replicas).astype(jnp.float32)
    total = jnp.concatenate(
        [
            lax.dynamic_index_in_dim(total, chip_at(replica, core, table, place), 0, True)
            for place in range(replicas // 2)
        ],
        axis=0,
    )
    turns = len(table[0]).bit_length() - 1
    for turn in range(turns - 1, -1, -1):
        half = total.shape[0] // 2
        arrived = exchange(total[half:].astype(jnp.bfloat16), replicas, turn)
        total = total[:half] + arrived.astype(jnp.float32)
    return total[0]


def adam_update(weight_now, moment, second, gradient):
    moment_new = decay_first * moment + (1.0 - decay_first) * gradient
    second_new = decay_second * second + (1.0 - decay_second) * gradient * gradient
    update = (
        learn_rate
        * (moment_new / (1.0 - decay_first**step_count))
        / (jnp.sqrt(second_new / (1.0 - decay_second**step_count)) + adam_floor)
    )
    return (weight_now - update, moment_new, second_new)


WIDE = 512
GATHER = ("ac", "ba")
REDUCE = ("ac", "ac")


def call(kernel, outs, *args, scratch=(), flops=0, limit=12 << 20, after=(), aliases=None):
    moved = sum(math.prod(a.shape) * a.dtype.itemsize for a in args)
    moved += sum(math.prod(o.shape) * o.dtype.itemsize for o in outs)
    spaces = [pltpu.VMEM] * len(args)
    skipped = len(after)
    aliases = {skipped + source: target for source, target in (aliases or {}).items()}

    def body(*refs):
        kernel(*refs[skipped:])

    return pl.pallas_call(
        body,
        out_shape=outs,
        in_specs=[pl.BlockSpec(memory_space=space) for space in [pl.ANY] * skipped + spaces],
        out_specs=[pl.BlockSpec(memory_space=pltpu.VMEM)] * len(outs),
        scratch_shapes=scratch,
        input_output_aliases=aliases,
        compiler_params=pltpu.CompilerParams(vmem_limit_bytes=limit),
        cost_estimate=pl.CostEstimate(flops=flops, bytes_accessed=moved, transcendentals=0),
    )(*after, *args)


def spec(shape, kind):
    return jax.ShapeDtypeStruct(tuple(shape), kind)


def blocks_of(width):
    size = min(WIDE, width)
    return [slice(start, start + size) for start in range(0, width, size)]


def dot(left, right):
    return jnp.dot(left, right, preferred_element_type=jnp.float32)


def near_kernel(value, near):
    near[...] = value[...]


def expand(source, basis, tokens, expanded):
    width = expanded.shape[1]
    squares = 0.0
    for part in blocks_of(width):
        piece = dot(source, basis[:, part]) + tokens[:, part].astype(jnp.float32)
        expanded[:, part] = piece
        squares = squares + jnp.sum(piece * piece, axis=1, keepdims=True)
    return lax.rsqrt(squares * (1.0 / width) + epsilon)


def expand_kernel(source, basis, tokens, gain, expanded, normed, inverse):
    inv = expand(source[...], basis, tokens, expanded)
    inverse[...] = jnp.broadcast_to(inv, inverse.shape)
    for part in blocks_of(normed.shape[1]):
        normed[:, part] = (expanded[:, part] * inv * gain[:, part]).astype(jnp.bfloat16)


def act(both):
    width = both.shape[1] // 2
    gate, up = both[:, :width], both[:, width:]
    sigma = jax.nn.sigmoid(gate)
    return gate, up, sigma


def front(source, normed, w_gate_up, w_down):
    both = 0.0
    for part in blocks_of(normed.shape[1]):
        both = both + dot(normed[:, part], w_gate_up[part, :])
    gate, up, sigma = act(both)
    hidden = (gate * sigma * up).astype(jnp.bfloat16)
    output = (source.astype(jnp.float32) + dot(hidden, w_down[...])).astype(jnp.bfloat16)
    return both, hidden, output


def assemble(pieces, places, first, theirs, w_gate_up, w_down):
    rows = w_gate_up.shape[0] // (2 * places)
    extra = w_down.shape[0] // (2 * places)
    width = w_gate_up.shape[1] // 2
    up, packed = pieces
    for stream in range(2):
        targets = places_of(places, GATHER[stream])[places if theirs else 0 :]
        for place in range(up.shape[0]):
            target = targets[first + place]
            lines = pl.ds(pl.multiple_of(target * rows, rows), rows)
            if stream == 0:
                w_gate_up[lines, width:] = up[place]
                continue
            w_gate_up[lines, :width] = packed[place, :rows, :]
            lines = pl.ds(pl.multiple_of(target * extra, extra), extra)
            for turn, low in enumerate(range(rows, packed.shape[1], extra)):
                w_down[lines, turn * width : (turn + 1) * width] = packed[place, low : low + extra, :]


def early_kernel(*refs):
    *pieces, w_gate_up, w_down = refs
    half = pieces[0].shape[0]
    for index, theirs in enumerate((False, True)):
        assemble(pieces[2 * index : 2 * index + 2], 2 * half, 0, theirs, w_gate_up, w_down)


def own_kernel(up, packed, part_gate_up, part_down, w_gate_up, w_down):
    half = up.shape[0]
    assemble((up, packed), 2 * half, half, False, w_gate_up, w_down)


def front_kernel(up, packed, part_gate_up, part_down, normed, source, w_gate_up, w_down, both, hidden, *outputs):
    half = up.shape[0]
    assemble((up, packed), 2 * half, half, True, w_gate_up, w_down)
    count = source.shape[0] // len(outputs)

    @pl.when(lax.axis_index("section") == 0)
    def _():
        both[...], hidden[...], output = front(source[...], normed, w_gate_up, w_down)
        for index, out in enumerate(outputs):
            out[...] = output[index * count : (index + 1) * count]


def turn_kernel(*refs):
    half = len(refs) // 2
    for source, target in zip(refs[:half], refs[half:]):
        step = min(WIDE, source.shape[0])
        for low in range(0, source.shape[0], step):
            target[:, low : low + step] = source[low : low + step, :].T


def back(next_grad, both, expanded, inv, gain, gate_up_turned, down_turned, basis_turned, scaled):
    gate, up, sigma = act(both)
    hidden_grad = dot(next_grad, down_turned[...])
    gate_grad = (hidden_grad * up * (sigma * (1.0 + gate * (1.0 - sigma)))).astype(jnp.bfloat16)
    up_grad = (hidden_grad * (gate * sigma)).astype(jnp.bfloat16)
    grads = jnp.concatenate([gate_grad, up_grad], axis=1)
    width = expanded.shape[1]
    total = 0.0
    for part in blocks_of(width):
        piece = dot(grads, gate_up_turned[:, part]) * gain[:, part]
        scaled[:, part] = piece
        total = total + jnp.sum(piece * expanded[:, part], axis=1, keepdims=True)
    mean = total * inv * (1.0 / width)
    coord_grad = next_grad.astype(jnp.float32)
    for part in blocks_of(width):
        piece = inv * (scaled[:, part] - expanded[:, part] * inv * mean)
        coord_grad = coord_grad + dot(piece.astype(jnp.bfloat16), basis_turned[part, :])
    return gate_grad, coord_grad.astype(jnp.bfloat16)


def middle_kernel(
    batch, source, cotangent, basis, tokens, gain, w_gate_up, w_down,
    gate_up_turned, down_turned, basis_turned, output, coord_grad, normed, hidden, gate_grad, expanded, scaled,
):
    cot, tokens = cotangent.at[batch], tokens.at[batch]

    @pl.when(lax.axis_index("section") != 0)
    def _():
        start = source[...]
        inv = expand(start, basis, tokens, expanded)
        for part in blocks_of(normed.shape[1]):
            normed[:, part] = (expanded[:, part] * inv * gain[:, part]).astype(jnp.bfloat16)
        both, hidden[...], output[...] = front(start, normed, w_gate_up, w_down)
        gate_grad[...], coord_grad[...] = back(
            cot[...], both, expanded, inv, gain, gate_up_turned, down_turned, basis_turned, scaled
        )


def back_kernel(
    batch, next_grad, both, expanded, inverse, gain, gate_up_turned, down_turned, basis_turned,
    coord_grad, gate_grad, scaled,
):
    rows = pl.ds(batch * next_grad.shape[0], next_grad.shape[0])

    @pl.when(lax.axis_index("section") == 0)
    def _():
        gate_grad[...], coord_grad[...] = back(
            next_grad[...], both[rows, :], expanded.at[rows], inverse[rows, :1],
            gain, gate_up_turned, down_turned, basis_turned, scaled,
        )


def grads_kernel(*refs):
    *inputs, kept_a, kept_b, sent_a, sent_b, hidden, gate_grad, next_grad, down_all, turned = refs
    turned0, hidden0, cotangent, *inputs = inputs
    batches, count, _ = cotangent.shape
    places, _, width = kept_a.shape
    section = lax.axis_index("section")

    @pl.when(section == 0)
    def _():
        hidden[...] = hidden0[...]
        for batch in range(batches):
            rows = pl.ds(batch * count, count)
            next_grad[rows, :] = inputs[2 * batch][...]
            gate_grad[rows, :] = inputs[2 * batch + 1][...]

    @pl.when(section != 0)
    def _():
        for batch in range(batches):
            rows = pl.ds(batch * count, count)
            group = inputs[2 * batches + 3 * batch : 2 * batches + 3 * batch + 3]
            next_grad[rows, :] = cotangent[batch]
            hidden[rows, :] = group[1][...]
            gate_grad[rows, :] = group[2][...]
            for part in blocks_of(turned.shape[0]):
                turned[part, rows] = group[0][:, part].T

    down_all[...] = contract_first(hidden[...], next_grad[...])
    rows = turned.shape[0] // (2 * places)
    extra = down_all.shape[0] // (2 * places)
    cuts = cuts_of(rows + extra * (down_all.shape[1] // width))

    def fill(source):
        for index, target in enumerate(places_of(places, REDUCE[0])):
            blocks = (kept_a, kept_b) if index < places else (sent_a, sent_b)
            place = index % places
            lines = down_all[pl.ds(pl.multiple_of(target * extra, extra), extra), :]
            gate = dot(source[pl.ds(pl.multiple_of(target * rows, rows), rows), :], gate_grad[...])
            for cut, block in zip(cuts, blocks):
                top = min(cut.stop, rows)
                block[place, : top - cut.start, :] = gate[cut.start : top, :].astype(block.dtype)
                if cut.stop > rows:
                    for turn in range(lines.shape[1] // width):
                        low = top - cut.start + turn * extra
                        block[place, low : low + extra, :] = lines[
                            :, turn * width : (turn + 1) * width
                        ].astype(block.dtype)

    @pl.when(section == 0)
    def _():
        fill(turned0)

    @pl.when(section != 0)
    def _():
        fill(turned)


def cuts_of(rows):
    first = rows // 32 * 16
    return [slice(0, first), slice(first, rows)]


def places_of(places, kinds):
    replica = lax.axis_index("replica")
    core, chip = replica & 1, replica >> 1
    table = offsets(2 * places, kinds)
    result = []
    for which in (core, 1 - core):
        for low, high in zip(*table):
            result.append((chip ^ jnp.where(which == 0, low, high)) * 2 + which)
    return result


def select_kernel(*refs):
    *inputs, produced, returned = refs
    batches = produced.shape[1]
    section = lax.axis_index("section")
    for index, target in enumerate((produced, returned)):
        for batch in range(batches):
            first = inputs[2 * batches * index + batch]
            second = inputs[2 * batches * index + batches + batch]

            @pl.when(section == 0)
            def _(first=first, target=target, batch=batch):
                target[0, batch] = first[...]

            @pl.when(section != 0)
            def _(second=second, target=target, batch=batch):
                target[0, batch] = second[...]


def finish_kernel(scale, *refs):
    kept_a, kept_b, come_a, come_b, gw, gm, gs, dw, dm, ds, *outs = refs
    rows = gw.shape[1]
    extra = dw.shape[1]
    parts = [kept[0] + come[0].astype(jnp.float32) for kept, come in ((kept_a, come_a), (kept_b, come_b))]
    share = jnp.concatenate(parts, axis=0) * scale
    gate = share[:rows]
    down = jnp.concatenate(
        [share[low : low + extra] for low in range(rows, share.shape[0], extra)], axis=1
    )
    for values, grad, targets in (((gw, gm, gs), gate, outs[:3]), ((dw, dm, ds), down, outs[3:])):
        results = adam_update(*(value[0] for value in values), grad)
        for target, result in zip(targets, results):
            target[0] = result


def two_sections(
    coords_in, token_rows, cotangent, basis, gain, gate_weight, up_weight, down_weight,
    gate_moment, gate_second, down_moment, down_second,
):
    batches, rows, coord_width = coords_in.shape
    model_width = basis.shape[1]
    replicas = lax.axis_size("replica")
    share_rows, width = gate_weight.shape[1:]
    down_rows = down_weight.shape[1]
    bf16, f32 = jnp.bfloat16, jnp.float32
    hidden_width = down_rows * replicas
    full = batches * rows
    lines = [down_weight[0, :, low : low + width] for low in range(0, coord_width, width)]
    packed = jnp.concatenate([part.astype(bf16) for part in (gate_weight[0], *lines)], axis=0)
    (up_near,) = call(near_kernel, [spec(up_weight.shape, bf16)], up_weight)
    held = [up_near, packed[None]]
    turns = (replicas // 2).bit_length() - 1
    source = coords_in.reshape(full, coord_width)
    tokens = token_rows.reshape(full, model_width)
    expanded, normed, inverse = call(
        expand_kernel,
        [spec((full, model_width), f32), spec((full, model_width), bf16), spec((full, 128), f32)],
        source, basis, tokens, gain,
        flops=2 * full * coord_width * model_width,
    )
    for turn in range(turns):
        come = []
        for part, kinds, name in zip(held, GATHER, ("up", "packed")):
            sent = up_weight if turn == 0 and name == "up" else part
            come.append(exchange(sent, replicas, turn, kinds))
        if turn < turns - 1:
            held = [jnp.concatenate(pair, axis=0) for pair in zip(held, come)]
    theirs = []
    for part, name in zip(held, ("up", "packed")):
        theirs.append(swap_cores(part, replicas))
    last = [swap_cores(part, replicas) for part in come]
    weights = [spec((model_width, 2 * width), bf16), spec((hidden_width, coord_width), bf16)]
    parts = call(early_kernel, weights, *held, *theirs)
    part_gate_up, part_down = call(own_kernel, weights, *come, *parts, aliases={2: 0, 3: 1})
    row_out = spec((rows, coord_width), bf16)
    w_gate_up, w_down, both, hidden, *outputs = call(
        front_kernel,
        weights + [spec((full, 2 * width), f32), spec((full, width), bf16)] + [row_out] * batches,
        *last, part_gate_up, part_down, normed, source,
        flops=4 * full * width * model_width,
        aliases={2: 0, 3: 1},
    )
    incoming = [swap_sections(outputs[0])]
    turned = call(
        turn_kernel,
        [spec(value.shape[::-1], bf16) for value in (w_gate_up, w_down, basis, normed)],
        w_gate_up, w_down, basis, normed,
        limit=16 << 20,
    )
    later, turned = lax.optimization_barrier((outputs[1:], turned))
    incoming += [swap_sections(out) for out in later]
    *turned, normed_turned = turned
    made, grads, group1 = [], [], []
    for batch in range(batches):
        output, coord_grad, *kept = call(
            functools.partial(middle_kernel, batch),
            [row_out, row_out, spec((rows, model_width), bf16), spec((rows, width), bf16), spec((rows, width), bf16)],
            incoming[batch], cotangent, basis, token_rows, gain, w_gate_up, w_down, *turned,
            scratch=[pltpu.VMEM((rows, model_width), f32), pltpu.VMEM((rows, model_width), f32)],
            flops=8 * rows * coord_width * model_width,
            after=grads[-1:],
        )
        made.append(output)
        grads.append(coord_grad)
        group1 += kept
    arrived = [swap_sections(grad) for grad in grads]
    first_grads, group0 = [], []
    for batch in range(batches):
        coord_grad, gate_grad = call(
            functools.partial(back_kernel, batch), [row_out, spec((rows, width), bf16)],
            arrived[batch], both, expanded, inverse, gain, *turned,
            scratch=[pltpu.VMEM((rows, model_width), f32)],
            flops=4 * rows * coord_width * model_width,
            after=first_grads[-1:],
        )
        first_grads.append(coord_grad)
        group0 += [arrived[batch], gate_grad]
    cuts = cuts_of(share_rows + down_rows * (coord_width // width))
    shapes = [(replicas // 2, cut.stop - cut.start, width) for cut in cuts]
    blocks = call(
        grads_kernel, [spec(shape, kind) for kind in (f32, bf16) for shape in shapes],
        normed_turned, hidden, cotangent, *group0, *group1,
        scratch=[
            pltpu.VMEM((full, width), bf16), pltpu.VMEM((full, width), bf16),
            pltpu.VMEM((full, coord_width), bf16), pltpu.VMEM((hidden_width, coord_width), f32),
            pltpu.VMEM((model_width, full), bf16),
        ],
        flops=2 * full * width * (model_width + coord_width),
        limit=16 << 20,
    )
    swapped = [swap_cores(sent, replicas) for sent in blocks[2:]]
    totals = [kept + sent.astype(f32) for kept, sent in zip(blocks, swapped)]
    for turn in range(turns - 1, -1, -1):
        half = totals[0].shape[0] // 2
        come = [
            exchange(total[half:].astype(bf16), replicas, turn, kinds) for total, kinds in zip(totals, REDUCE)
        ]
        totals = [total[:half] for total in totals]
        if turn:
            totals = [total + part.astype(f32) for total, part in zip(totals, come)]
    produced, returned = call(
        select_kernel, [spec((1,) + coords_in.shape, bf16)] * 2, *outputs, *made, *first_grads, *grads
    )
    grad_scale = 1.0 / math.sqrt(full * replicas)
    weights = (gate_weight, gate_moment, gate_second, down_weight, down_moment, down_second)
    updated = call(
        functools.partial(finish_kernel, grad_scale),
        [spec(weight.shape, f32) for weight in weights],
        *totals, *come, *weights,
    )
    return (produced, returned, *updated)


def per_device(
    coords_in,
    token_rows,
    cotangent,
    subspace_basis,
    norm_gain,
    gate_weight,
    up_weight,
    down_weight,
    gate_moment,
    gate_second,
    down_moment,
    down_second,
):
    batches, rows_dev, coord_width = coords_in.shape
    model_width = subspace_basis.shape[1]
    sections = lax.axis_size("section")
    replicas = lax.axis_size("replica")
    section = lax.axis_index("section")
    share_rows, hidden_width = gate_weight.shape[1:]
    down_rows = down_weight.shape[1]
    bf16 = jnp.bfloat16

    gate_up = jnp.concatenate([gate_weight[0].astype(bf16), up_weight[0]], axis=1)
    down = down_weight[0].astype(bf16)
    packed = jnp.concatenate([gate_up, down.reshape(-1, gate_up.shape[1])], axis=0)
    gathered = gather_shares(packed)
    w_gate_up = gathered[:, :share_rows].reshape(model_width, 2 * hidden_width)
    w_down = gathered[:, share_rows:].reshape(hidden_width, coord_width)

    def put(buffer, item, slot):
        return lax.dynamic_update_index_in_dim(buffer, item, slot, 0)

    def get(buffer, slot):
        return lax.dynamic_index_in_dim(buffer, slot, 0, False)

    def room(*dims, kind=bf16):
        return jnp.zeros((batches + 1, rows_dev) + dims, kind)

    store = {
        "output": room(coord_width),
        "expanded": room(model_width, kind=jnp.float32),
        "inverse": room(1, kind=jnp.float32),
        "normed": room(model_width),
        "gate": room(hidden_width, kind=jnp.float32),
        "up": room(hidden_width, kind=jnp.float32),
        "hidden": room(hidden_width),
        "returned": room(coord_width),
        "next_grad": room(coord_width),
        "gate_grad": room(hidden_width),
    }
    blank = jnp.zeros((rows_dev, coord_width), bf16)

    def forward(tick, incoming):
        batch = tick - section
        slot = jnp.clip(batch, 0, batches)
        read = jnp.clip(batch, 0, batches - 1)
        source = jnp.where(section == 0, get(coords_in, read), incoming)
        expanded = jnp.dot(source, subspace_basis, preferred_element_type=jnp.float32) + get(
            token_rows, read
        ).astype(jnp.float32)
        inverse = lax.rsqrt(jnp.mean(expanded * expanded, axis=1, keepdims=True) + epsilon)
        normed = (expanded * inverse * norm_gain).astype(bf16)
        both = jnp.dot(normed, w_gate_up, preferred_element_type=jnp.float32)
        gate, up = both[:, :hidden_width], both[:, hidden_width:]
        hidden = (gate * jax.nn.sigmoid(gate) * up).astype(bf16)
        output = (
            source.astype(jnp.float32)
            + jnp.dot(hidden, w_down, preferred_element_type=jnp.float32)
        ).astype(bf16)
        for name, item in (
            ("output", output),
            ("expanded", expanded),
            ("inverse", inverse),
            ("normed", normed),
            ("gate", gate),
            ("up", up),
            ("hidden", hidden),
        ):
            store[name] = put(store[name], item, slot)
        return shift(output, "section", 1)

    def backward(tick, incoming):
        batch = tick - (sections - 1 - section)
        live = (batch >= 0) & (batch < batches)
        slot = jnp.clip(batch, 0, batches)
        read = jnp.clip(batch, 0, batches - 1)
        next_grad = jnp.where(section == sections - 1, get(cotangent, read), incoming)
        next_grad = jnp.where(live, next_grad, jnp.zeros_like(next_grad))
        gate, up = get(store["gate"], read), get(store["up"], read)
        expanded, inverse = get(store["expanded"], read), get(store["inverse"], read)
        hidden_grad = contract_last(next_grad, w_down)
        sigma = jax.nn.sigmoid(gate)
        gate_grad = (hidden_grad * up * (sigma * (1.0 + gate * (1.0 - sigma)))).astype(bf16)
        up_grad = (hidden_grad * (gate * sigma)).astype(bf16)
        normed_grad = contract_last(jnp.concatenate([gate_grad, up_grad], axis=1), w_gate_up)
        scaled = normed_grad * norm_gain
        centred = expanded * inverse
        expanded_grad = (
            inverse * (scaled - centred * jnp.mean(scaled * centred, axis=1, keepdims=True))
        ).astype(bf16)
        coord_grad = (
            next_grad.astype(jnp.float32) + contract_last(expanded_grad, subspace_basis)
        ).astype(bf16)
        for name, item in (
            ("returned", coord_grad),
            ("next_grad", next_grad),
            ("gate_grad", gate_grad),
        ):
            store[name] = put(store[name], item, slot)
        return shift(coord_grad, "section", -1)

    ticks = sections + batches - 1
    down_stream, up_stream = blank, blank
    for tick in range(ticks + sections - 1):
        if tick < ticks:
            down_stream = forward(tick, down_stream)
        if tick >= sections - 1:
            up_stream = backward(tick - (sections - 1), up_stream)

    def flat(name):
        return store[name][:batches].reshape(batches * rows_dev, -1)

    gate_sum = contract_first(flat("normed"), flat("gate_grad")).astype(bf16)
    down_sum = contract_first(flat("hidden"), flat("next_grad")).astype(bf16)
    down_sum = down_sum.reshape(replicas, down_rows, coord_width)
    pieces = [gate_sum.reshape(replicas, share_rows, hidden_width)]
    for start in range(0, coord_width, hidden_width):
        pieces.append(down_sum[:, :, start : start + hidden_width])
    share = reduce_shares(jnp.concatenate(pieces, axis=1))
    gate_share = share[:share_rows]
    down_share = jnp.concatenate(
        [
            share[start : start + down_rows]
            for start in range(share_rows, share.shape[0], down_rows)
        ],
        axis=1,
    )
    grad_scale = 1.0 / math.sqrt(batches * rows_dev * replicas)
    gate_new, gate_moment_new, gate_second_new = adam_update(
        gate_weight[0], gate_moment[0], gate_second[0], gate_share * grad_scale
    )
    down_new, down_moment_new, down_second_new = adam_update(
        down_weight[0], down_moment[0], down_second[0], down_share * grad_scale
    )
    return (
        store["output"][None, :batches],
        store["returned"][None, :batches],
        gate_new[None],
        gate_moment_new[None],
        gate_second_new[None],
        down_new[None],
        down_moment_new[None],
        down_second_new[None],
    )


def solution(mesh):
    rows = P(None, "replica", None)
    weight = P("section", "replica", None)
    stacked = P("section", None, "replica", None)
    two = mesh.shape["section"] == 2

    def body(*values):
        return (two_sections if two else per_device)(*values)

    return jax.shard_map(
        body,
        mesh=mesh,
        in_specs=(rows, rows, rows, P(), P("section", None)) + (weight,) * 7,
        out_specs=(stacked, stacked) + (weight,) * 6,
        check_vma=False,
    )
```

profile of v0, /device:TPU:0, one launch (start us, length us, event | category | flops | bytes accessed | tf_op | source)
XLA Modules:
  0.0 68.0 jit_solution(10863476423818700576)
XLA Ops:
  2.5 3.0 %collective-permute-start.4 = (bf16[1,160,256]{2,1,0:T(8,128)(2,1)S(1)}, bf16[1,160,256]{2,1,0:T(8,128)(2,1)S(1)}, u32[]{:S(2)}, u32[]{:S(2)}) collective-permute-start(bf16[1,160,256]{2,1,0:T(8,128)(2,1)S(1)} %maximum_bitcast_fusion), channel_id=1, source_target_pairs={{0,2},{1,9},{2,0},{3,11},{4,6},{5,13},{6,4},{7,15},{8,10},{9,1},{1... | collective-permute-start | bytes 245768 | tf_op jit(solution)/shard_map/ppermute | solution.py:48
  5.5 2.6 %collective-permute-start = (bf16[1,128,256]{2,1,0:T(8,128)(2,1)}, bf16[1,128,256]{2,1,0:T(8,128)(2,1)S(1)}, u32[]{:S(2)}, u32[]{:S(2)}) collective-permute-start(bf16[1,128,256]{2,1,0:T(8,128)(2,1)} %refs_0_.1), channel_id=1, source_target_pairs={{0,8},{1,9},{2,10},{3,11},{4,12},{5,13},{6,14},{7,15},{8,0},{9,1},... | collective-permute-start | bytes 196616 | tf_op jit(solution)/shard_map/ppermute | solution.py:48
  8.1 3.0 %collective-permute-start.5 = (bf16[2,160,256]{2,1,0:T(8,128)(2,1)S(1)}, bf16[2,160,256]{2,1,0:T(8,128)(2,1)S(1)}, u32[]{:S(2)}, u32[]{:S(2)}) collective-permute-start(bf16[2,160,256]{2,1,0:T(8,128)(2,1)S(1)} %pad_maximum_fusion.2), channel_id=1, source_target_pairs={{0,8},{1,5},{2,10},{3,7},{4,12},{5,1},{6,14},{7,3},{8,0},{9,13},{1... | collective-permute-start | bytes 491528 | tf_op jit(solution)/shard_map/ppermute | solution.py:48
  13.7 1.3 %collective-permute-done.5 = bf16[2,160,256]{2,1,0:T(8,128)(2,1)S(1)} collective-permute-done((bf16[2,160,256]{2,1,0:T(8,128)(2,1)S(1)}, bf16[2,160,256]{2,1,0:T(8,128)(2,1)S(1)}, u32[]{:S(2)}, u32[]{:S(2)}) %collective-permute-start.5) | collective-permute-done | bytes 163872 | tf_op jit(solution)/shard_map/ppermute | solution.py:48
  15.0 3.2 %collective-permute-start.6 = (bf16[4,160,256]{2,1,0:T(8,128)(2,1)S(1)}, bf16[4,160,256]{2,1,0:T(8,128)(2,1)S(1)}, u32[]{:S(2)}, u32[]{:S(2)}) collective-permute-start(bf16[4,160,256]{2,1,0:T(8,128)(2,1)S(1)} %pad_maximum_fusion.refs_1_), channel_id=1, source_target_pairs={{0,4},{1,3},{2,6},{3,1},{4,0},{5,7},{6,2},{7,5},{8,12},{9,11},{10,... | collective-permute-start | bytes 983048 | tf_op jit(solution)/shard_map/ppermute | solution.py:48
  18.2 1.1 %collective-permute-start.2 = (bf16[4,128,256]{2,1,0:T(8,128)(2,1)S(1)}, bf16[4,128,256]{2,1,0:T(8,128)(2,1)S(1)}, u32[]{:S(2)}, u32[]{:S(2)}) collective-permute-start(bf16[4,128,256]{2,1,0:T(8,128)(2,1)S(1)} %pad_maximum_fusion.1.refs_0_), channel_id=1, source_target_pairs={{0,2},{1,5},{2,0},{3,7},{4,6},{5,1},{6,4},{7,3},{8,10},{9,13},{10,... | collective-permute-start | bytes 786440 | tf_op jit(solution)/shard_map/ppermute | solution.py:48
  19.3 6.7 %collective-permute-done.6.refs_1_ = bf16[4,160,256]{2,1,0:T(8,128)(2,1)S(1)} collective-permute-done((bf16[4,160,256]{2,1,0:T(8,128)(2,1)S(1)}, bf16[4,160,256]{2,1,0:T(8,128)(2,1)S(1)}, u32[]{:S(2)}, u32[]{:S(2)}) %collective-permute-start.6) | collective-permute-done | bytes 327712 | tf_op jit(solution)/shard_map/ppermute | solution.py:48
  26.6 1.2 %copy-done.1 = bf16[2,128,2048]{2,1,0:T(8,128)(2,1)S(1)} copy-done((bf16[2,128,2048]{2,1,0:T(8,128)(2,1)S(1)}, bf16[2,128,2048]{2,1,0:T(8,128)(2,1)}, u32[]{:S(2)}) %copy-start.1) | copy-done | bytes 1048600
  31.6 1.5 %shard_map.184 = (bf16[512,2048]{1,0:T(8,128)(2,1)S(1)}, bf16[512,256]{1,0:T(8,128)(2,1)S(1)}, bf16[2048,512]{1,0:T(8,128)(2,1)S(1)}, bf16[2048,256]{1,0:T(8,128)(2,1)S(1)}) custom-call(bf16[2048,512]{1,0:T(8,128)(2,1)S(1)} %get-tuple-element.63.refs_0_.refs_5_.refs_6_, bf16[256,512]{1,0:T(8,128)(2,1)S(1)} %get-tuple-element.64.refs_1_.refs_6_.refs_7_, ...), custom_call_target="tpu_custom_call" | custom-call | bytes 11010048 | tf_op jit(solution)/shard_map/pallas_call | solution.py:141
  33.1 1.4 %collective-permute-start.11 = (bf16[128,512]{1,0:T(8,128)(2,1)S(1)}, bf16[128,512]{1,0:T(8,128)(2,1)S(1)}, u32[]{:S(2)}, u32[]{:S(2)}) collective-permute-start(bf16[128,512]{1,0:T(8,128)(2,1)S(1)} %get-tuple-element.74.refs_1_), channel_id=1, source_target_pairs={{0,16},{16,0},{1,17},{17,1},{2,18},{18,2},{3,19},{19,3},{4,20},{20... | collective-permute-start | bytes 393224 | tf_op jit(solution)/shard_map/ppermute | solution.py:52
  34.5 2.8 %collective-permute-done.10.refs_0_ = bf16[128,512]{1,0:T(8,128)(2,1)S(1)} collective-permute-done((bf16[128,512]{1,0:T(8,128)(2,1)S(1)}, bf16[128,512]{1,0:T(8,128)(2,1)S(1)}, u32[]{:S(2)}, u32[]{:S(2)}) %collective-permute-start.10) | collective-permute-done | bytes 131104 | tf_op jit(solution)/shard_map/ppermute | solution.py:52
  37.3 2.6 %collective-permute-start.12 = (bf16[128,512]{1,0:T(8,128)(2,1)S(1)}, bf16[128,512]{1,0:T(8,128)(2,1)S(1)}, u32[]{:S(2)}, u32[]{:S(2)}) collective-permute-start(bf16[128,512]{1,0:T(8,128)(2,1)S(1)} %get-tuple-element.73.refs_0_.refs_6_), channel_id=1, source_target_pairs={{0,16},{16,0},{1,17},{17,1},{2,18},{18,2},{3,19},{19,3},{4,20},{20... | collective-permute-start | bytes 393224 | tf_op jit(solution)/shard_map/ppermute | solution.py:52
  39.9 2.7 %collective-permute-start.13 = (bf16[128,512]{1,0:T(8,128)(2,1)S(1)}, bf16[128,512]{1,0:T(8,128)(2,1)S(1)}, u32[]{:S(2)}, u32[]{:S(2)}) collective-permute-start(bf16[128,512]{1,0:T(8,128)(2,1)S(1)} %get-tuple-element.80.refs_7_), channel_id=1, source_target_pairs={{0,16},{16,0},{1,17},{17,1},{2,18},{18,2},{3,19},{19,3},{4,20},{20... | collective-permute-start | bytes 393224 | tf_op jit(solution)/shard_map/ppermute | solution.py:52
  43.2 1.2 %shard_map.187 = (bf16[128,512]{1,0:T(8,128)(2,1)S(1)}, bf16[128,256]{1,0:T(8,128)(2,1)S(1)}) custom-call(bf16[128,512]{1,0:T(8,128)(2,1)S(1)} %collective-permute-done.12.refs_0_.refs_3_, f32[256,512]{1,0:T(8,128)S(1)} %get-tuple-element.76.refs_1_.refs_2_, f32[256,2048]{1,0:T(8,128)S(1)} %get-tuple-element.77.refs_2_.refs_3_, ...), custom_call_target="tpu_custom_call" | custom-call | flops 536870912 | bytes 7544832 | tf_op jit(solution)/shard_map/pallas_call | solution.py:141
  44.4 1.5 %collective-permute-done.13.refs_1_.refs_5_ = bf16[128,512]{1,0:T(8,128)(2,1)S(1)} collective-permute-done((bf16[128,512]{1,0:T(8,128)(2,1)S(1)}, bf16[128,512]{1,0:T(8,128)(2,1)S(1)}, u32[]{:S(2)}, u32[]{:S(2)}) %collective-permute-start.13) | collective-permute-done | bytes 131104 | tf_op jit(solution)/shard_map/ppermute | solution.py:52
  45.8 1.2 %shard_map.188 = (bf16[128,512]{1,0:T(8,128)(2,1)S(1)}, bf16[128,256]{1,0:T(8,128)(2,1)S(1)}) custom-call(bf16[128,512]{1,0:T(8,128)(2,1)S(1)} %get-tuple-element.79.refs_0_.refs_4_, bf16[128,512]{1,0:T(8,128)(2,1)S(1)} %collective-permute-done.13.refs_1_.refs_5_, f32[256,512]{1,0:T(8,128)S(1)} %get-tuple-element.76.refs_1_.refs_2_, ...), custom_call_target="tpu_custom_call" | custom-call | flops 536870912 | bytes 7544832 | tf_op jit(solution)/shard_map/pallas_call | solution.py:141
  48.3 1.1 %collective-permute-done.14 = bf16[8,80,256]{2,1,0:T(8,128)(2,1)S(1)} collective-permute-done((bf16[8,80,256]{2,1,0:T(8,128)(2,1)S(1)}, bf16[8,80,256]{2,1,0:T(8,128)(2,1)S(1)}, u32[]{:S(2)}, u32[]{:S(2)}) %collective-permute-start.14) | collective-permute-done | bytes 327712 | tf_op jit(solution)/shard_map/ppermute | solution.py:56
  49.5 1.3 %collective-permute-start.15 = (bf16[4,80,256]{2,1,0:T(8,128)(2,1)S(1)}, bf16[4,80,256]{2,1,0:T(8,128)(2,1)S(1)}, u32[]{:S(2)}, u32[]{:S(2)}) collective-permute-start(bf16[4,80,256]{2,1,0:T(8,128)(2,1)S(1)} %slice.91), channel_id=1, source_target_pairs={{0,2},{1,5},{2,0},{3,7},{4,6},{5,1},{6,4},{7,3},{8,10},{9,13},{10,... | collective-permute-start | bytes 491528 | tf_op jit(solution)/shard_map/ppermute | solution.py:48
  51.9 3.1 %collective-permute-done.15 = bf16[4,80,256]{2,1,0:T(8,128)(2,1)S(1)} collective-permute-done((bf16[4,80,256]{2,1,0:T(8,128)(2,1)S(1)}, bf16[4,80,256]{2,1,0:T(8,128)(2,1)S(1)}, u32[]{:S(2)}, u32[]{:S(2)}) %collective-permute-start.15) | collective-permute-done | bytes 163872 | tf_op jit(solution)/shard_map/ppermute | solution.py:48
  55.0 2.1 %collective-permute-start.16 = (bf16[2,80,256]{2,1,0:T(8,128)(2,1)S(1)}, bf16[2,80,256]{2,1,0:T(8,128)(2,1)S(1)}, u32[]{:S(2)}, u32[]{:S(2)}) collective-permute-start(bf16[2,80,256]{2,1,0:T(8,128)(2,1)S(1)} %slice.93), channel_id=1, source_target_pairs={{0,4},{1,3},{2,6},{3,1},{4,0},{5,7},{6,2},{7,5},{8,12},{9,11},{10,... | collective-permute-start | bytes 245768 | tf_op jit(solution)/shard_map/ppermute | solution.py:48
  57.1 1.7 %collective-permute-start.19 = (bf16[2,80,256]{2,1,0:T(8,128)(2,1)S(1)}, bf16[2,80,256]{2,1,0:T(8,128)(2,1)S(1)}, u32[]{:S(2)}, u32[]{:S(2)}) collective-permute-start(bf16[2,80,256]{2,1,0:T(8,128)(2,1)S(1)} %slice.92), channel_id=1, source_target_pairs={{0,4},{1,3},{2,6},{3,1},{4,0},{5,7},{6,2},{7,5},{8,12},{9,11},{10,... | collective-permute-start | bytes 245768 | tf_op jit(solution)/shard_map/ppermute | solution.py:48
  59.5 2.5 %collective-permute-start.20 = (bf16[1,80,256]{2,1,0:T(8,128)(2,1)S(1)}, bf16[1,80,256]{2,1,0:T(8,128)(2,1)S(1)}, u32[]{:S(2)}, u32[]{:S(2)}) collective-permute-start(bf16[1,80,256]{2,1,0:T(8,128)(2,1)S(1)} %slice.95), channel_id=1, source_target_pairs={{0,8},{1,9},{2,10},{3,11},{4,12},{5,13},{6,14},{7,15},{8,0},{9,1},... | collective-permute-start | bytes 122888 | tf_op jit(solution)/shard_map/ppermute | solution.py:48
  62.1 2.5 %collective-permute-start.21 = (bf16[1,80,256]{2,1,0:T(8,128)(2,1)S(1)}, bf16[1,80,256]{2,1,0:T(8,128)(2,1)S(1)}, u32[]{:S(2)}, u32[]{:S(2)}) collective-permute-start(bf16[1,80,256]{2,1,0:T(8,128)(2,1)S(1)} %slice.94), channel_id=1, source_target_pairs={{0,8},{1,9},{2,10},{3,11},{4,12},{5,13},{6,14},{7,15},{8,0},{9,1},... | collective-permute-start | bytes 122888 | tf_op jit(solution)/shard_map/ppermute | solution.py:48
  65.5 1.6 %collective-permute-done.21.refs_3_ = bf16[1,80,256]{2,1,0:T(8,128)(2,1)S(1)} collective-permute-done((bf16[1,80,256]{2,1,0:T(8,128)(2,1)S(1)}, bf16[1,80,256]{2,1,0:T(8,128)(2,1)S(1)}, u32[]{:S(2)}, u32[]{:S(2)}) %collective-permute-start.21) | collective-permute-done | bytes 40992 | tf_op jit(solution)/shard_map/ppermute | solution.py:48
  (81 shorter events, 14.2 us)
Async XLA Ops:
  0.6 25.9 %copy-start.6 = (f32[1,2048]{1,0:T(1,128)S(1)}, f32[1,2048]{1,0:T(1,128)}, u32[]{:S(2)}) copy-start(f32[1,2048]{1,0:T(1,128)} %refs_5_.4) | copy-start | bytes 24580
  0.6 25.9 %copy-start = (bf16[512,2048]{1,0:T(8,128)(2,1)S(1)}, bf16[512,2048]{1,0:T(8,128)(2,1)}, u32[]{:S(2)}) copy-start(bf16[512,2048]{1,0:T(8,128)(2,1)} %refs_3_.5) | copy-start | bytes 6291460
  2.5 5.6 %collective-permute-start.4 = (bf16[1,160,256]{2,1,0:T(8,128)(2,1)S(1)}, bf16[1,160,256]{2,1,0:T(8,128)(2,1)S(1)}, u32[]{:S(2)}, u32[]{:S(2)}) collective-permute-start(bf16[1,160,256]{2,1,0:T(8,128)(2,1)S(1)} %maximum_bitcast_fusion), channel_id=1, source_target_pairs={{0,2},{1,9},{2,0},{3,11},{4,6},{5,13},{6,4},{7,15},{8,10},{9,1},{1... | collective-permute-start | bytes 245768 | tf_op jit(solution)/shard_map/ppermute | solution.py:48
  5.5 7.3 %collective-permute-start = (bf16[1,128,256]{2,1,0:T(8,128)(2,1)}, bf16[1,128,256]{2,1,0:T(8,128)(2,1)S(1)}, u32[]{:S(2)}, u32[]{:S(2)}) collective-permute-start(bf16[1,128,256]{2,1,0:T(8,128)(2,1)} %refs_0_.1), channel_id=1, source_target_pairs={{0,8},{1,9},{2,10},{3,11},{4,12},{5,13},{6,14},{7,15},{8,0},{9,1},... | collective-permute-start | bytes 196616 | tf_op jit(solution)/shard_map/ppermute | solution.py:48
  8.1 6.8 %collective-permute-start.5 = (bf16[2,160,256]{2,1,0:T(8,128)(2,1)S(1)}, bf16[2,160,256]{2,1,0:T(8,128)(2,1)S(1)}, u32[]{:S(2)}, u32[]{:S(2)}) collective-permute-start(bf16[2,160,256]{2,1,0:T(8,128)(2,1)S(1)} %pad_maximum_fusion.2), channel_id=1, source_target_pairs={{0,8},{1,5},{2,10},{3,7},{4,12},{5,1},{6,14},{7,3},{8,0},{9,13},{1... | collective-permute-start | bytes 491528 | tf_op jit(solution)/shard_map/ppermute | solution.py:48
  12.8 5.4 %collective-permute-start.1 = (bf16[2,128,256]{2,1,0:T(8,128)(2,1)S(1)}, bf16[2,128,256]{2,1,0:T(8,128)(2,1)S(1)}, u32[]{:S(2)}, u32[]{:S(2)}) collective-permute-start(bf16[2,128,256]{2,1,0:T(8,128)(2,1)S(1)} %pad_maximum_fusion.3), channel_id=1, source_target_pairs={{0,4},{1,3},{2,6},{3,1},{4,0},{5,7},{6,2},{7,5},{8,12},{9,11},{10,... | collective-permute-start | bytes 393224 | tf_op jit(solution)/shard_map/ppermute | solution.py:48
  15.0 11.0 %collective-permute-start.6 = (bf16[4,160,256]{2,1,0:T(8,128)(2,1)S(1)}, bf16[4,160,256]{2,1,0:T(8,128)(2,1)S(1)}, u32[]{:S(2)}, u32[]{:S(2)}) collective-permute-start(bf16[4,160,256]{2,1,0:T(8,128)(2,1)S(1)} %pad_maximum_fusion.refs_1_), channel_id=1, source_target_pairs={{0,4},{1,3},{2,6},{3,1},{4,0},{5,7},{6,2},{7,5},{8,12},{9,11},{10,... | collective-permute-start | bytes 983048 | tf_op jit(solution)/shard_map/ppermute | solution.py:48
  18.2 8.3 %collective-permute-start.2 = (bf16[4,128,256]{2,1,0:T(8,128)(2,1)S(1)}, bf16[4,128,256]{2,1,0:T(8,128)(2,1)S(1)}, u32[]{:S(2)}, u32[]{:S(2)}) collective-permute-start(bf16[4,128,256]{2,1,0:T(8,128)(2,1)S(1)} %pad_maximum_fusion.1.refs_0_), channel_id=1, source_target_pairs={{0,2},{1,5},{2,0},{3,7},{4,6},{5,1},{6,4},{7,3},{8,10},{9,13},{10,... | collective-permute-start | bytes 786440 | tf_op jit(solution)/shard_map/ppermute | solution.py:48
  19.3 10.4 %collective-permute-start.9 = (bf16[4,160,256]{2,1,0:T(8,128)(2,1)S(1)}, bf16[4,160,256]{2,1,0:T(8,128)(2,1)S(1)}, u32[]{:S(2)}, u32[]{:S(2)}) collective-permute-start(bf16[4,160,256]{2,1,0:T(8,128)(2,1)S(1)} %pad_maximum_fusion.refs_1_), channel_id=1, source_target_pairs={{0,1},{1,0},{2,3},{3,2},{4,5},{5,4},{6,7},{7,6},{8,9},{9,8},{10,11... | collective-permute-start | bytes 983048 | tf_op jit(solution)/shard_map/ppermute | solution.py:56
  26.0 3.9 %collective-permute-start.7 = (bf16[4,160,256]{2,1,0:T(8,128)(2,1)S(1)}, bf16[4,160,256]{2,1,0:T(8,128)(2,1)S(1)}, u32[]{:S(2)}, u32[]{:S(2)}) collective-permute-start(bf16[4,160,256]{2,1,0:T(8,128)(2,1)S(1)} %collective-permute-done.6.refs_1_), channel_id=1, source_target_pairs={{0,1},{1,0},{2,3},{3,2},{4,5},{5,4},{6,7},{7,6},{8,9},{9,8},{10,11... | collective-permute-start | bytes 983048 | tf_op jit(solution)/shard_map/ppermute | solution.py:56
  26.1 3.6 %collective-permute-start.8 = (bf16[4,128,256]{2,1,0:T(8,128)(2,1)S(1)}, bf16[4,128,256]{2,1,0:T(8,128)(2,1)S(1)}, u32[]{:S(2)}, u32[]{:S(2)}) collective-permute-start(bf16[4,128,256]{2,1,0:T(8,128)(2,1)S(1)} %pad_maximum_fusion.1.refs_0_), channel_id=1, source_target_pairs={{0,1},{1,0},{2,3},{3,2},{4,5},{5,4},{6,7},{7,6},{8,9},{9,8},{10,11... | collective-permute-start | bytes 786440 | tf_op jit(solution)/shard_map/ppermute | solution.py:56
  26.6 3.3 %collective-permute-start.3 = (bf16[4,128,256]{2,1,0:T(8,128)(2,1)S(1)}, bf16[4,128,256]{2,1,0:T(8,128)(2,1)S(1)}, u32[]{:S(2)}, u32[]{:S(2)}) collective-permute-start(bf16[4,128,256]{2,1,0:T(8,128)(2,1)S(1)} %collective-permute-done.2.refs_0_), channel_id=1, source_target_pairs={{0,1},{1,0},{2,3},{3,2},{4,5},{5,4},{6,7},{7,6},{8,9},{9,8},{10,11... | collective-permute-start | bytes 786440 | tf_op jit(solution)/shard_map/ppermute | solution.py:56
  30.8 6.4 %collective-permute-start.10 = (bf16[128,512]{1,0:T(8,128)(2,1)S(1)}, bf16[128,512]{1,0:T(8,128)(2,1)S(1)}, u32[]{:S(2)}, u32[]{:S(2)}) collective-permute-start(bf16[128,512]{1,0:T(8,128)(2,1)S(1)} %get-tuple-element.61.refs_0_), channel_id=1, source_target_pairs={{0,16},{16,0},{1,17},{17,1},{2,18},{18,2},{3,19},{19,3},{4,20},{20... | collective-permute-start | bytes 393224 | tf_op jit(solution)/shard_map/ppermute | solution.py:52
  33.1 6.8 %collective-permute-start.11 = (bf16[128,512]{1,0:T(8,128)(2,1)S(1)}, bf16[128,512]{1,0:T(8,128)(2,1)S(1)}, u32[]{:S(2)}, u32[]{:S(2)}) collective-permute-start(bf16[128,512]{1,0:T(8,128)(2,1)S(1)} %get-tuple-element.74.refs_1_), channel_id=1, source_target_pairs={{0,16},{16,0},{1,17},{17,1},{2,18},{18,2},{3,19},{19,3},{4,20},{20... | collective-permute-start | bytes 393224 | tf_op jit(solution)/shard_map/ppermute | solution.py:52
  37.3 5.9 %collective-permute-start.12 = (bf16[128,512]{1,0:T(8,128)(2,1)S(1)}, bf16[128,512]{1,0:T(8,128)(2,1)S(1)}, u32[]{:S(2)}, u32[]{:S(2)}) collective-permute-start(bf16[128,512]{1,0:T(8,128)(2,1)S(1)} %get-tuple-element.73.refs_0_.refs_6_), channel_id=1, source_target_pairs={{0,16},{16,0},{1,17},{17,1},{2,18},{18,2},{3,19},{19,3},{4,20},{20... | collective-permute-start | bytes 393224 | tf_op jit(solution)/shard_map/ppermute | solution.py:52
  39.9 6.0 %collective-permute-start.13 = (bf16[128,512]{1,0:T(8,128)(2,1)S(1)}, bf16[128,512]{1,0:T(8,128)(2,1)S(1)}, u32[]{:S(2)}, u32[]{:S(2)}) collective-permute-start(bf16[128,512]{1,0:T(8,128)(2,1)S(1)} %get-tuple-element.80.refs_7_), channel_id=1, source_target_pairs={{0,16},{16,0},{1,17},{17,1},{2,18},{18,2},{3,19},{19,3},{4,20},{20... | collective-permute-start | bytes 393224 | tf_op jit(solution)/shard_map/ppermute | solution.py:52
  47.7 1.7 %collective-permute-start.14 = (bf16[8,80,256]{2,1,0:T(8,128)(2,1)S(1)}, bf16[8,80,256]{2,1,0:T(8,128)(2,1)S(1)}, u32[]{:S(2)}, u32[]{:S(2)}) collective-permute-start(bf16[8,80,256]{2,1,0:T(8,128)(2,1)S(1)} %get-tuple-element.95), channel_id=1, source_target_pairs={{0,1},{1,0},{2,3},{3,2},{4,5},{5,4},{6,7},{7,6},{8,9},{9,8},{10,11... | collective-permute-start | bytes 983048 | tf_op jit(solution)/shard_map/ppermute | solution.py:56
  47.8 3.0 %collective-permute-start.17 = (bf16[8,80,256]{2,1,0:T(8,128)(2,1)S(1)}, bf16[8,80,256]{2,1,0:T(8,128)(2,1)S(1)}, u32[]{:S(2)}, u32[]{:S(2)}) collective-permute-start(bf16[8,80,256]{2,1,0:T(8,128)(2,1)S(1)} %get-tuple-element.97), channel_id=1, source_target_pairs={{0,1},{1,0},{2,3},{3,2},{4,5},{5,4},{6,7},{7,6},{8,9},{9,8},{10,11... | collective-permute-start | bytes 983048 | tf_op jit(solution)/shard_map/ppermute | solution.py:56
  49.5 5.4 %collective-permute-start.15 = (bf16[4,80,256]{2,1,0:T(8,128)(2,1)S(1)}, bf16[4,80,256]{2,1,0:T(8,128)(2,1)S(1)}, u32[]{:S(2)}, u32[]{:S(2)}) collective-permute-start(bf16[4,80,256]{2,1,0:T(8,128)(2,1)S(1)} %slice.91), channel_id=1, source_target_pairs={{0,2},{1,5},{2,0},{3,7},{4,6},{5,1},{6,4},{7,3},{8,10},{9,13},{10,... | collective-permute-start | bytes 491528 | tf_op jit(solution)/shard_map/ppermute | solution.py:48
  51.0 6.1 %collective-permute-start.18 = (bf16[4,80,256]{2,1,0:T(8,128)(2,1)S(1)}, bf16[4,80,256]{2,1,0:T(8,128)(2,1)S(1)}, u32[]{:S(2)}, u32[]{:S(2)}) collective-permute-start(bf16[4,80,256]{2,1,0:T(8,128)(2,1)S(1)} %slice.90), channel_id=1, source_target_pairs={{0,2},{1,5},{2,0},{3,7},{4,6},{5,1},{6,4},{7,3},{8,10},{9,13},{10,... | collective-permute-start | bytes 491528 | tf_op jit(solution)/shard_map/ppermute | solution.py:48
  55.0 4.5 %collective-permute-start.16 = (bf16[2,80,256]{2,1,0:T(8,128)(2,1)S(1)}, bf16[2,80,256]{2,1,0:T(8,128)(2,1)S(1)}, u32[]{:S(2)}, u32[]{:S(2)}) collective-permute-start(bf16[2,80,256]{2,1,0:T(8,128)(2,1)S(1)} %slice.93), channel_id=1, source_target_pairs={{0,4},{1,3},{2,6},{3,1},{4,0},{5,7},{6,2},{7,5},{8,12},{9,11},{10,... | collective-permute-start | bytes 245768 | tf_op jit(solution)/shard_map/ppermute | solution.py:48
  57.1 4.9 %collective-permute-start.19 = (bf16[2,80,256]{2,1,0:T(8,128)(2,1)S(1)}, bf16[2,80,256]{2,1,0:T(8,128)(2,1)S(1)}, u32[]{:S(2)}, u32[]{:S(2)}) collective-permute-start(bf16[2,80,256]{2,1,0:T(8,128)(2,1)S(1)} %slice.92), channel_id=1, source_target_pairs={{0,4},{1,3},{2,6},{3,1},{4,0},{5,7},{6,2},{7,5},{8,12},{9,11},{10,... | collective-permute-start | bytes 245768 | tf_op jit(solution)/shard_map/ppermute | solution.py:48
  59.5 6.0 %collective-permute-start.20 = (bf16[1,80,256]{2,1,0:T(8,128)(2,1)S(1)}, bf16[1,80,256]{2,1,0:T(8,128)(2,1)S(1)}, u32[]{:S(2)}, u32[]{:S(2)}) collective-permute-start(bf16[1,80,256]{2,1,0:T(8,128)(2,1)S(1)} %slice.95), channel_id=1, source_target_pairs={{0,8},{1,9},{2,10},{3,11},{4,12},{5,13},{6,14},{7,15},{8,0},{9,1},... | collective-permute-start | bytes 122888 | tf_op jit(solution)/shard_map/ppermute | solution.py:48
  62.1 5.0 %collective-permute-start.21 = (bf16[1,80,256]{2,1,0:T(8,128)(2,1)S(1)}, bf16[1,80,256]{2,1,0:T(8,128)(2,1)S(1)}, u32[]{:S(2)}, u32[]{:S(2)}) collective-permute-start(bf16[1,80,256]{2,1,0:T(8,128)(2,1)S(1)} %slice.94), channel_id=1, source_target_pairs={{0,8},{1,9},{2,10},{3,11},{4,12},{5,13},{6,14},{7,15},{8,0},{9,1},... | collective-permute-start | bytes 122888 | tf_op jit(solution)/shard_map/ppermute | solution.py:48
  (11 other events, 111.3 us)
where the time goes:
time: 68.2 us; the launch traced here: 68 us
  starting transfers between devices  33.3 us (49%)
  waiting for transfers between devices  20.1 us (29%)
  Pallas kernels  8.27 us (12%)
  local copies, waits for them, and re-layouts  3.16 us (5%)
  other arithmetic  2.16 us (3%)
  between operations  0.97 us (1%)
    ppermute x12, starting transfers between devices, exchange(): return lax.ppermute(value, 'replica', pairs)  24.8 us
    ppermute x12, waiting for transfers between devices, exchange(): return lax.ppermute(value, 'replica', pairs)  14.1 us
    pallas_call x13, Pallas kernels, call(): pl.pallas_call(body, out_shape=outs, in_specs=[pl.BlockSpec(memory_space=...  8.27 us
    ppermute x4, starting transfers between devices, swap_sections(): return lax.ppermute(value, 'section', [(0, 1), (1, 0)])  7.39 us
    ppermute x4, waiting for transfers between devices, swap_sections(): return lax.ppermute(value, 'section', [(0, 1), (1, 0)])  4.89 us
    unnamed x26, local copies, waits for them, and re-layouts  3.06 us
  transfers between devices with their start and end apart: 22, of which 10 were waited for; matrix products, arithmetic and copies ran while one was open for 1% of the time, Pallas kernels for 7%

commit v1 on v0

--- a/solution.py
+++ b/solution.py
@@ -252,11 +252,16 @@
             target[:, low : low + step] = source[low : low + step, :].T
 
 
-def back(next_grad, both, expanded, inv, gain, gate_up_turned, down_turned, basis_turned, scaled):
+def inner(next_grad, both, down_turned):
     gate, up, sigma = act(both)
     hidden_grad = dot(next_grad, down_turned[...])
     gate_grad = (hidden_grad * up * (sigma * (1.0 + gate * (1.0 - sigma)))).astype(jnp.bfloat16)
     up_grad = (hidden_grad * (gate * sigma)).astype(jnp.bfloat16)
+    return gate_grad, up_grad
+
+
+def back(next_grad, both, expanded, inv, gain, gate_up_turned, down_turned, basis_turned, scaled):
+    gate_grad, up_grad = inner(next_grad, both, down_turned)
     grads = jnp.concatenate([gate_grad, up_grad], axis=1)
     width = expanded.shape[1]
     total = 0.0
@@ -290,18 +295,30 @@
         )
 
 
-def back_kernel(
-    batch, next_grad, both, expanded, inverse, gain, gate_up_turned, down_turned, basis_turned,
-    coord_grad, gate_grad, scaled,
-):
+def inner_kernel(batch, next_grad, both, down_turned, gate_grad):
     rows = pl.ds(batch * next_grad.shape[0], next_grad.shape[0])
 
     @pl.when(lax.axis_index("section") == 0)
     def _():
-        gate_grad[...], coord_grad[...] = back(
-            next_grad[...], both[rows, :], expanded.at[rows], inverse[rows, :1],
+        gate_grad[...] = inner(next_grad[...], both[rows, :], down_turned)[0]
+
+
+def back_kernel(*refs):
+    both, expanded, inverse, gain, gate_up_turned, down_turned, basis_turned, *refs = refs
+    *values, next_grad, scaled = refs
+    half = len(values) // 2
+
+    @pl.when(lax.axis_index("section") == 0)
+    def _():
+        count = values[0].shape[0]
+        for batch in range(half):
+            next_grad[pl.ds(batch * count, count), :] = values[batch][...]
+        coord_grad = back(
+            next_grad[...], both[...], expanded, inverse[:, :1],
             gain, gate_up_turned, down_turned, basis_turned, scaled,
-        )
+        )[1]
+        for batch in range(half):
+            values[half + batch][...] = coord_grad[batch * count : (batch + 1) * count]
 
 
 def grads_kernel(*refs):
@@ -480,18 +497,24 @@
         made.append(output)
         grads.append(coord_grad)
         group1 += kept
-    arrived = [swap_sections(grad) for grad in grads]
-    first_grads, group0 = [], []
+    arrived = []
+    for grad in grads:
+        arrived.append(swap_sections(grad))
+    group0 = []
     for batch in range(batches):
-        coord_grad, gate_grad = call(
-            functools.partial(back_kernel, batch), [row_out, spec((rows, width), bf16)],
-            arrived[batch], both, expanded, inverse, gain, *turned,
-            scratch=[pltpu.VMEM((rows, model_width), f32)],
-            flops=4 * rows * coord_width * model_width,
-            after=first_grads[-1:],
+        (gate_grad,) = call(
+            functools.partial(inner_kernel, batch), [spec((rows, width), bf16)],
+            arrived[batch], both, turned[1],
+            flops=2 * rows * coord_width * width,
+            after=group0[-1:],
         )
-        first_grads.append(coord_grad)
         group0 += [arrived[batch], gate_grad]
+    first_grads = call(
+        back_kernel, [row_out] * batches,
+        both, expanded, inverse, gain, *turned, *arrived,
+        scratch=[pltpu.VMEM((full, coord_width), bf16), pltpu.VMEM((full, model_width), f32)],
+        flops=4 * full * coord_width * model_width,
+    )
     cuts = cuts_of(share_rows + down_rows * (coord_width // width))
     shapes = [(replicas // 2, cut.stop - cut.start, width) for cut in cuts]
     blocks = call(
@@ -509,9 +532,9 @@
     totals = [kept + sent.astype(f32) for kept, sent in zip(blocks, swapped)]
     for turn in range(turns - 1, -1, -1):
         half = totals[0].shape[0] // 2
-        come = [
-            exchange(total[half:].astype(bf16), replicas, turn, kinds) for total, kinds in zip(totals, REDUCE)
-        ]
+        come = []
+        for total, kinds in zip(totals, REDUCE):
+            come.append(exchange(total[half:].astype(bf16), replicas, turn, kinds))
         totals = [total[:half] for total in totals]
         if turn:
             totals = [total + part.astype(f32) for total, part in zip(totals, come)]

time: 68.2 us -> 67.5 us (0.990)
    ppermute x12, waiting for transfers between devices: 14.1 us -> 12.6 us  [exchange(): return lax.ppermute(value, 'replica', pairs)]
    ppermute x4, waiting for transfers between devices: 4.89 us -> 5.84 us  [swap_sections(): return lax.ppermute(value, 'section', [(0, 1), (1, 0)])]
    pallas_call x13 -> x14, Pallas kernels: 8.27 us -> 8.09 us  [call(): pl.pallas_call(body, out_shape=outs, in_specs=[pl.BlockSpec(memory_space=...]
  transfers between devices with their start and end apart: 22 -> 22, of which waited for: 10 -> 9; matrix products, arithmetic and copies ran while one was open for 1% -> 1% of each run, Pallas kernels for 7% -> 8%
where the time goes in v1:
time: 67.5 us; the launch traced here: 67.3 us
  starting transfers between devices  33.3 us (49%)
  waiting for transfers between devices  19.6 us (29%)
  Pallas kernels  8.09 us (12%)
  local copies, waits for them, and re-layouts  3.14 us (5%)
  other arithmetic  2.16 us (3%)
  between operations  0.98 us (1%)
    ppermute x12, starting transfers between devices, exchange(): return lax.ppermute(value, 'replica', pairs)  24.8 us
    ppermute x12, waiting for transfers between devices, exchange(): return lax.ppermute(value, 'replica', pairs)  12.6 us
    pallas_call x14, Pallas kernels, call(): pl.pallas_call(body, out_shape=outs, in_specs=[pl.BlockSpec(memory_space=...  8.09 us
    ppermute x4, starting transfers between devices, swap_sections(): return lax.ppermute(value, 'section', [(0, 1), (1, 0)])  7.4 us
    ppermute x4, waiting for transfers between devices, swap_sections(): return lax.ppermute(value, 'section', [(0, 1), (1, 0)])  5.84 us
    unnamed x26, local copies, waits for them, and re-layouts  3.05 us
  transfers between devices with their start and end apart: 22, of which 9 were waited for; matrix products, arithmetic and copies ran while one was open for 1% of the time, Pallas kernels for 8%

profile of v1, /device:TPU:0, one launch (start us, length us, event | category | flops | bytes accessed | tf_op | source)
XLA Modules:
  0.0 67.3 jit_solution(12799877096563651545)
XLA Ops:
  2.5 3.0 %collective-permute-start.4 = (bf16[1,160,256]{2,1,0:T(8,128)(2,1)S(1)}, bf16[1,160,256]{2,1,0:T(8,128)(2,1)S(1)}, u32[]{:S(2)}, u32[]{:S(2)}) collective-permute-start(bf16[1,160,256]{2,1,0:T(8,128)(2,1)S(1)} %maximum_bitcast_fusion), channel_id=1, source_target_pairs={{0,2},{1,9},{2,0},{3,11},{4,6},{5,13},{6,4},{7,15},{8,10},{9,1},{1... | collective-permute-start | bytes 245768 | tf_op jit(solution)/shard_map/ppermute | solution.py:48
  5.5 2.6 %collective-permute-start = (bf16[1,128,256]{2,1,0:T(8,128)(2,1)}, bf16[1,128,256]{2,1,0:T(8,128)(2,1)S(1)}, u32[]{:S(2)}, u32[]{:S(2)}) collective-permute-start(bf16[1,128,256]{2,1,0:T(8,128)(2,1)} %refs_0_.1), channel_id=1, source_target_pairs={{0,8},{1,9},{2,10},{3,11},{4,12},{5,13},{6,14},{7,15},{8,0},{9,1},... | collective-permute-start | bytes 196616 | tf_op jit(solution)/shard_map/ppermute | solution.py:48
  8.1 3.0 %collective-permute-start.5 = (bf16[2,160,256]{2,1,0:T(8,128)(2,1)S(1)}, bf16[2,160,256]{2,1,0:T(8,128)(2,1)S(1)}, u32[]{:S(2)}, u32[]{:S(2)}) collective-permute-start(bf16[2,160,256]{2,1,0:T(8,128)(2,1)S(1)} %pad_maximum_fusion.2), channel_id=1, source_target_pairs={{0,8},{1,5},{2,10},{3,7},{4,12},{5,1},{6,14},{7,3},{8,0},{9,13},{1... | collective-permute-start | bytes 491528 | tf_op jit(solution)/shard_map/ppermute | solution.py:48
  13.7 1.3 %collective-permute-done.5 = bf16[2,160,256]{2,1,0:T(8,128)(2,1)S(1)} collective-permute-done((bf16[2,160,256]{2,1,0:T(8,128)(2,1)S(1)}, bf16[2,160,256]{2,1,0:T(8,128)(2,1)S(1)}, u32[]{:S(2)}, u32[]{:S(2)}) %collective-permute-start.5) | collective-permute-done | bytes 163872 | tf_op jit(solution)/shard_map/ppermute | solution.py:48
  15.0 3.2 %collective-permute-start.6 = (bf16[4,160,256]{2,1,0:T(8,128)(2,1)S(1)}, bf16[4,160,256]{2,1,0:T(8,128)(2,1)S(1)}, u32[]{:S(2)}, u32[]{:S(2)}) collective-permute-start(bf16[4,160,256]{2,1,0:T(8,128)(2,1)S(1)} %pad_maximum_fusion.refs_1_), channel_id=1, source_target_pairs={{0,4},{1,3},{2,6},{3,1},{4,0},{5,7},{6,2},{7,5},{8,12},{9,11},{10,... | collective-permute-start | bytes 983048 | tf_op jit(solution)/shard_map/ppermute | solution.py:48
  18.2 1.1 %collective-permute-start.2 = (bf16[4,128,256]{2,1,0:T(8,128)(2,1)S(1)}, bf16[4,128,256]{2,1,0:T(8,128)(2,1)S(1)}, u32[]{:S(2)}, u32[]{:S(2)}) collective-permute-start(bf16[4,128,256]{2,1,0:T(8,128)(2,1)S(1)} %pad_maximum_fusion.1.refs_0_), channel_id=1, source_target_pairs={{0,2},{1,5},{2,0},{3,7},{4,6},{5,1},{6,4},{7,3},{8,10},{9,13},{10,... | collective-permute-start | bytes 786440 | tf_op jit(solution)/shard_map/ppermute | solution.py:48
  19.3 6.7 %collective-permute-done.6.refs_1_ = bf16[4,160,256]{2,1,0:T(8,128)(2,1)S(1)} collective-permute-done((bf16[4,160,256]{2,1,0:T(8,128)(2,1)S(1)}, bf16[4,160,256]{2,1,0:T(8,128)(2,1)S(1)}, u32[]{:S(2)}, u32[]{:S(2)}) %collective-permute-start.6) | collective-permute-done | bytes 327712 | tf_op jit(solution)/shard_map/ppermute | solution.py:48
  26.6 1.2 %copy-done.1 = bf16[2,128,2048]{2,1,0:T(8,128)(2,1)S(1)} copy-done((bf16[2,128,2048]{2,1,0:T(8,128)(2,1)S(1)}, bf16[2,128,2048]{2,1,0:T(8,128)(2,1)}, u32[]{:S(2)}) %copy-start.1) | copy-done | bytes 1048600
  27.8 0.9 %copy-done.4 = bf16[2,128,512]{2,1,0:T(8,128)(2,1)S(1)} copy-done((bf16[2,128,512]{2,1,0:T(8,128)(2,1)S(1)}, bf16[2,128,512]{2,1,0:T(8,128)(2,1)}, u32[]{:S(2)}) %copy-start.4) | copy-done | bytes 262168
  28.8 0.9 %shard_map.182 = (f32[256,2048]{1,0:T(8,128)S(1)}, bf16[256,2048]{1,0:T(8,128)(2,1)S(1)}, f32[256,128]{1,0:T(8,128)S(1)}) custom-call(bf16[256,512]{1,0:T(8,128)(2,1)S(1)} %bitcast.11, bf16[512,2048]{1,0:T(8,128)(2,1)S(1)} %copy-done, bf16[256,2048]{1,0:T(8,128)(2,1)S(1)} %bitcast.10, f32[1,2048]{1,0:T(1,128)S(1)} %copy-done.9), custom_call_target="tpu_custom_call" | custom-call | flops 536870912 | bytes 6692864 | tf_op jit(solution)/shard_map/pallas_call | solution.py:141
  31.6 1.5 %shard_map.184 = (bf16[512,2048]{1,0:T(8,128)(2,1)S(1)}, bf16[512,256]{1,0:T(8,128)(2,1)S(1)}, bf16[2048,512]{1,0:T(8,128)(2,1)S(1)}, bf16[2048,256]{1,0:T(8,128)(2,1)S(1)}) custom-call(bf16[2048,512]{1,0:T(8,128)(2,1)S(1)} %get-tuple-element.61.refs_0_.refs_5_.refs_6_, bf16[256,512]{1,0:T(8,128)(2,1)S(1)} %get-tuple-element.62.refs_1_.refs_6_.refs_7_, ...), custom_call_target="tpu_custom_call" | custom-call | bytes 11010048 | tf_op jit(solution)/shard_map/pallas_call | solution.py:141
  33.1 1.4 %collective-permute-start.11 = (bf16[128,512]{1,0:T(8,128)(2,1)S(1)}, bf16[128,512]{1,0:T(8,128)(2,1)S(1)}, u32[]{:S(2)}, u32[]{:S(2)}) collective-permute-start(bf16[128,512]{1,0:T(8,128)(2,1)S(1)} %get-tuple-element.72.refs_1_), channel_id=1, source_target_pairs={{0,16},{16,0},{1,17},{17,1},{2,18},{18,2},{3,19},{19,3},{4,20},{20... | collective-permute-start | bytes 393224 | tf_op jit(solution)/shard_map/ppermute | solution.py:52
  34.5 2.8 %collective-permute-done.10.refs_0_ = bf16[128,512]{1,0:T(8,128)(2,1)S(1)} collective-permute-done((bf16[128,512]{1,0:T(8,128)(2,1)S(1)}, bf16[128,512]{1,0:T(8,128)(2,1)S(1)}, u32[]{:S(2)}, u32[]{:S(2)}) %collective-permute-start.10) | collective-permute-done | bytes 131104 | tf_op jit(solution)/shard_map/ppermute | solution.py:52
  37.3 2.6 %collective-permute-start.12 = (bf16[128,512]{1,0:T(8,128)(2,1)S(1)}, bf16[128,512]{1,0:T(8,128)(2,1)S(1)}, u32[]{:S(2)}, u32[]{:S(2)}) collective-permute-start(bf16[128,512]{1,0:T(8,128)(2,1)S(1)} %get-tuple-element.71.refs_0_.refs_6_), channel_id=1, source_target_pairs={{0,16},{16,0},{1,17},{17,1},{2,18},{18,2},{3,19},{19,3},{4,20},{20... | collective-permute-start | bytes 393224 | tf_op jit(solution)/shard_map/ppermute | solution.py:52
  39.9 2.7 %collective-permute-start.13 = (bf16[128,512]{1,0:T(8,128)(2,1)S(1)}, bf16[128,512]{1,0:T(8,128)(2,1)S(1)}, u32[]{:S(2)}, u32[]{:S(2)}) collective-permute-start(bf16[128,512]{1,0:T(8,128)(2,1)S(1)} %get-tuple-element.77.refs_7_), channel_id=1, source_target_pairs={{0,16},{16,0},{1,17},{17,1},{2,18},{18,2},{3,19},{19,3},{4,20},{20... | collective-permute-start | bytes 393224 | tf_op jit(solution)/shard_map/ppermute | solution.py:52
  43.3 2.5 %collective-permute-done.13.refs_8_.refs_1_.refs_5_ = bf16[128,512]{1,0:T(8,128)(2,1)S(1)} collective-permute-done((bf16[128,512]{1,0:T(8,128)(2,1)S(1)}, bf16[128,512]{1,0:T(8,128)(2,1)S(1)}, u32[]{:S(2)}, u32[]{:S(2)}) %collective-permute-start.13) | collective-permute-done | bytes 131104 | tf_op jit(solution)/shard_map/ppermute | solution.py:52
  47.3 1.1 %collective-permute-done.14 = bf16[8,80,256]{2,1,0:T(8,128)(2,1)S(1)} collective-permute-done((bf16[8,80,256]{2,1,0:T(8,128)(2,1)S(1)}, bf16[8,80,256]{2,1,0:T(8,128)(2,1)S(1)}, u32[]{:S(2)}, u32[]{:S(2)}) %collective-permute-start.14) | collective-permute-done | bytes 327712 | tf_op jit(solution)/shard_map/ppermute | solution.py:56
  48.5 1.3 %collective-permute-start.15 = (bf16[4,80,256]{2,1,0:T(8,128)(2,1)S(1)}, bf16[4,80,256]{2,1,0:T(8,128)(2,1)S(1)}, u32[]{:S(2)}, u32[]{:S(2)}) collective-permute-start(bf16[4,80,256]{2,1,0:T(8,128)(2,1)S(1)} %slice.91), channel_id=1, source_target_pairs={{0,2},{1,5},{2,0},{3,7},{4,6},{5,1},{6,4},{7,3},{8,10},{9,13},{10,... | collective-permute-start | bytes 491528 | tf_op jit(solution)/shard_map/ppermute | solution.py:48
  50.8 3.1 %collective-permute-done.15 = bf16[4,80,256]{2,1,0:T(8,128)(2,1)S(1)} collective-permute-done((bf16[4,80,256]{2,1,0:T(8,128)(2,1)S(1)}, bf16[4,80,256]{2,1,0:T(8,128)(2,1)S(1)}, u32[]{:S(2)}, u32[]{:S(2)}) %collective-permute-start.15) | collective-permute-done | bytes 163872 | tf_op jit(solution)/shard_map/ppermute | solution.py:48
  54.0 2.1 %collective-permute-start.16 = (bf16[2,80,256]{2,1,0:T(8,128)(2,1)S(1)}, bf16[2,80,256]{2,1,0:T(8,128)(2,1)S(1)}, u32[]{:S(2)}, u32[]{:S(2)}) collective-permute-start(bf16[2,80,256]{2,1,0:T(8,128)(2,1)S(1)} %slice.93), channel_id=1, source_target_pairs={{0,4},{1,3},{2,6},{3,1},{4,0},{5,7},{6,2},{7,5},{8,12},{9,11},{10,... | collective-permute-start | bytes 245768 | tf_op jit(solution)/shard_map/ppermute | solution.py:48
  56.1 1.7 %collective-permute-start.19 = (bf16[2,80,256]{2,1,0:T(8,128)(2,1)S(1)}, bf16[2,80,256]{2,1,0:T(8,128)(2,1)S(1)}, u32[]{:S(2)}, u32[]{:S(2)}) collective-permute-start(bf16[2,80,256]{2,1,0:T(8,128)(2,1)S(1)} %slice.92), channel_id=1, source_target_pairs={{0,4},{1,3},{2,6},{3,1},{4,0},{5,7},{6,2},{7,5},{8,12},{9,11},{10,... | collective-permute-start | bytes 245768 | tf_op jit(solution)/shard_map/ppermute | solution.py:48
  58.5 2.5 %collective-permute-start.20 = (bf16[1,80,256]{2,1,0:T(8,128)(2,1)S(1)}, bf16[1,80,256]{2,1,0:T(8,128)(2,1)S(1)}, u32[]{:S(2)}, u32[]{:S(2)}) collective-permute-start(bf16[1,80,256]{2,1,0:T(8,128)(2,1)S(1)} %slice.95), channel_id=1, source_target_pairs={{0,8},{1,9},{2,10},{3,11},{4,12},{5,13},{6,14},{7,15},{8,0},{9,1},... | collective-permute-start | bytes 122888 | tf_op jit(solution)/shard_map/ppermute | solution.py:48
  61.1 2.5 %collective-permute-start.21 = (bf16[1,80,256]{2,1,0:T(8,128)(2,1)S(1)}, bf16[1,80,256]{2,1,0:T(8,128)(2,1)S(1)}, u32[]{:S(2)}, u32[]{:S(2)}) collective-permute-start(bf16[1,80,256]{2,1,0:T(8,128)(2,1)S(1)} %slice.94), channel_id=1, source_target_pairs={{0,8},{1,9},{2,10},{3,11},{4,12},{5,13},{6,14},{7,15},{8,0},{9,1},... | collective-permute-start | bytes 122888 | tf_op jit(solution)/shard_map/ppermute | solution.py:48
  63.7 1.7 %shard_map.187 = (bf16[128,512]{1,0:T(8,128)(2,1)S(1)}, bf16[128,512]{1,0:T(8,128)(2,1)S(1)}) custom-call(f32[256,512]{1,0:T(8,128)S(1)} %get-tuple-element.74.refs_0_.refs_1_.refs_2_, f32[256,2048]{1,0:T(8,128)S(1)} %get-tuple-element.75.refs_1_, f32[256,128]{1,0:T(8,128)S(1)} %get-tuple-element.76.refs_2_, f32[1,2048]{1,0:T(1,128)S(1)} %copy-done.9, ...), custom_call_target="tpu_custom_call" | custom-call | flops 1073741824 | bytes 7741440 | tf_op jit(solution)/shard_map/pallas_call | solution.py:141
  (82 shorter events, 12.7 us)
Async XLA Ops:
  0.6 25.9 %copy-start.9 = (f32[1,2048]{1,0:T(1,128)S(1)}, f32[1,2048]{1,0:T(1,128)}, u32[]{:S(2)}) copy-start(f32[1,2048]{1,0:T(1,128)} %refs_3_.7) | copy-start | bytes 24580
  0.6 25.9 %copy-start = (bf16[512,2048]{1,0:T(8,128)(2,1)S(1)}, bf16[512,2048]{1,0:T(8,128)(2,1)}, u32[]{:S(2)}) copy-start(bf16[512,2048]{1,0:T(8,128)(2,1)} %refs_3_.6) | copy-start | bytes 6291460
  2.5 5.6 %collective-permute-start.4 = (bf16[1,160,256]{2,1,0:T(8,128)(2,1)S(1)}, bf16[1,160,256]{2,1,0:T(8,128)(2,1)S(1)}, u32[]{:S(2)}, u32[]{:S(2)}) collective-permute-start(bf16[1,160,256]{2,1,0:T(8,128)(2,1)S(1)} %maximum_bitcast_fusion), channel_id=1, source_target_pairs={{0,2},{1,9},{2,0},{3,11},{4,6},{5,13},{6,4},{7,15},{8,10},{9,1},{1... | collective-permute-start | bytes 245768 | tf_op jit(solution)/shard_map/ppermute | solution.py:48
  5.5 7.3 %collective-permute-start = (bf16[1,128,256]{2,1,0:T(8,128)(2,1)}, bf16[1,128,256]{2,1,0:T(8,128)(2,1)S(1)}, u32[]{:S(2)}, u32[]{:S(2)}) collective-permute-start(bf16[1,128,256]{2,1,0:T(8,128)(2,1)} %refs_0_.1), channel_id=1, source_target_pairs={{0,8},{1,9},{2,10},{3,11},{4,12},{5,13},{6,14},{7,15},{8,0},{9,1},... | collective-permute-start | bytes 196616 | tf_op jit(solution)/shard_map/ppermute | solution.py:48
  8.1 6.8 %collective-permute-start.5 = (bf16[2,160,256]{2,1,0:T(8,128)(2,1)S(1)}, bf16[2,160,256]{2,1,0:T(8,128)(2,1)S(1)}, u32[]{:S(2)}, u32[]{:S(2)}) collective-permute-start(bf16[2,160,256]{2,1,0:T(8,128)(2,1)S(1)} %pad_maximum_fusion.2), channel_id=1, source_target_pairs={{0,8},{1,5},{2,10},{3,7},{4,12},{5,1},{6,14},{7,3},{8,0},{9,13},{1... | collective-permute-start | bytes 491528 | tf_op jit(solution)/shard_map/ppermute | solution.py:48
  12.8 5.4 %collective-permute-start.1 = (bf16[2,128,256]{2,1,0:T(8,128)(2,1)S(1)}, bf16[2,128,256]{2,1,0:T(8,128)(2,1)S(1)}, u32[]{:S(2)}, u32[]{:S(2)}) collective-permute-start(bf16[2,128,256]{2,1,0:T(8,128)(2,1)S(1)} %pad_maximum_fusion.3), channel_id=1, source_target_pairs={{0,4},{1,3},{2,6},{3,1},{4,0},{5,7},{6,2},{7,5},{8,12},{9,11},{10,... | collective-permute-start | bytes 393224 | tf_op jit(solution)/shard_map/ppermute | solution.py:48
  15.0 11.0 %collective-permute-start.6 = (bf16[4,160,256]{2,1,0:T(8,128)(2,1)S(1)}, bf16[4,160,256]{2,1,0:T(8,128)(2,1)S(1)}, u32[]{:S(2)}, u32[]{:S(2)}) collective-permute-start(bf16[4,160,256]{2,1,0:T(8,128)(2,1)S(1)} %pad_maximum_fusion.refs_1_), channel_id=1, source_target_pairs={{0,4},{1,3},{2,6},{3,1},{4,0},{5,7},{6,2},{7,5},{8,12},{9,11},{10,... | collective-permute-start | bytes 983048 | tf_op jit(solution)/shard_map/ppermute | solution.py:48
  18.2 8.3 %collective-permute-start.2 = (bf16[4,128,256]{2,1,0:T(8,128)(2,1)S(1)}, bf16[4,128,256]{2,1,0:T(8,128)(2,1)S(1)}, u32[]{:S(2)}, u32[]{:S(2)}) collective-permute-start(bf16[4,128,256]{2,1,0:T(8,128)(2,1)S(1)} %pad_maximum_fusion.1.refs_0_), channel_id=1, source_target_pairs={{0,2},{1,5},{2,0},{3,7},{4,6},{5,1},{6,4},{7,3},{8,10},{9,13},{10,... | collective-permute-start | bytes 786440 | tf_op jit(solution)/shard_map/ppermute | solution.py:48
  19.3 10.4 %collective-permute-start.9 = (bf16[4,160,256]{2,1,0:T(8,128)(2,1)S(1)}, bf16[4,160,256]{2,1,0:T(8,128)(2,1)S(1)}, u32[]{:S(2)}, u32[]{:S(2)}) collective-permute-start(bf16[4,160,256]{2,1,0:T(8,128)(2,1)S(1)} %pad_maximum_fusion.refs_1_), channel_id=1, source_target_pairs={{0,1},{1,0},{2,3},{3,2},{4,5},{5,4},{6,7},{7,6},{8,9},{9,8},{10,11... | collective-permute-start | bytes 983048 | tf_op jit(solution)/shard_map/ppermute | solution.py:56
  26.0 3.9 %collective-permute-start.7 = (bf16[4,160,256]{2,1,0:T(8,128)(2,1)S(1)}, bf16[4,160,256]{2,1,0:T(8,128)(2,1)S(1)}, u32[]{:S(2)}, u32[]{:S(2)}) collective-permute-start(bf16[4,160,256]{2,1,0:T(8,128)(2,1)S(1)} %collective-permute-done.6.refs_1_), channel_id=1, source_target_pairs={{0,1},{1,0},{2,3},{3,2},{4,5},{5,4},{6,7},{7,6},{8,9},{9,8},{10,11... | collective-permute-start | bytes 983048 | tf_op jit(solution)/shard_map/ppermute | solution.py:56
  26.1 3.6 %collective-permute-start.8 = (bf16[4,128,256]{2,1,0:T(8,128)(2,1)S(1)}, bf16[4,128,256]{2,1,0:T(8,128)(2,1)S(1)}, u32[]{:S(2)}, u32[]{:S(2)}) collective-permute-start(bf16[4,128,256]{2,1,0:T(8,128)(2,1)S(1)} %pad_maximum_fusion.1.refs_0_), channel_id=1, source_target_pairs={{0,1},{1,0},{2,3},{3,2},{4,5},{5,4},{6,7},{7,6},{8,9},{9,8},{10,11... | collective-permute-start | bytes 786440 | tf_op jit(solution)/shard_map/ppermute | solution.py:56
  26.6 3.3 %collective-permute-start.3 = (bf16[4,128,256]{2,1,0:T(8,128)(2,1)S(1)}, bf16[4,128,256]{2,1,0:T(8,128)(2,1)S(1)}, u32[]{:S(2)}, u32[]{:S(2)}) collective-permute-start(bf16[4,128,256]{2,1,0:T(8,128)(2,1)S(1)} %collective-permute-done.2.refs_0_), channel_id=1, source_target_pairs={{0,1},{1,0},{2,3},{3,2},{4,5},{5,4},{6,7},{7,6},{8,9},{9,8},{10,11... | collective-permute-start | bytes 786440 | tf_op jit(solution)/shard_map/ppermute | solution.py:56
  30.8 6.4 %collective-permute-start.10 = (bf16[128,512]{1,0:T(8,128)(2,1)S(1)}, bf16[128,512]{1,0:T(8,128)(2,1)S(1)}, u32[]{:S(2)}, u32[]{:S(2)}) collective-permute-start(bf16[128,512]{1,0:T(8,128)(2,1)S(1)} %get-tuple-element.59.refs_0_), channel_id=1, source_target_pairs={{0,16},{16,0},{1,17},{17,1},{2,18},{18,2},{3,19},{19,3},{4,20},{20... | collective-permute-start | bytes 393224 | tf_op jit(solution)/shard_map/ppermute | solution.py:52
  33.1 6.8 %collective-permute-start.11 = (bf16[128,512]{1,0:T(8,128)(2,1)S(1)}, bf16[128,512]{1,0:T(8,128)(2,1)S(1)}, u32[]{:S(2)}, u32[]{:S(2)}) collective-permute-start(bf16[128,512]{1,0:T(8,128)(2,1)S(1)} %get-tuple-element.72.refs_1_), channel_id=1, source_target_pairs={{0,16},{16,0},{1,17},{17,1},{2,18},{18,2},{3,19},{19,3},{4,20},{20... | collective-permute-start | bytes 393224 | tf_op jit(solution)/shard_map/ppermute | solution.py:52
  37.3 5.9 %collective-permute-start.12 = (bf16[128,512]{1,0:T(8,128)(2,1)S(1)}, bf16[128,512]{1,0:T(8,128)(2,1)S(1)}, u32[]{:S(2)}, u32[]{:S(2)}) collective-permute-start(bf16[128,512]{1,0:T(8,128)(2,1)S(1)} %get-tuple-element.71.refs_0_.refs_6_), channel_id=1, source_target_pairs={{0,16},{16,0},{1,17},{17,1},{2,18},{18,2},{3,19},{19,3},{4,20},{20... | collective-permute-start | bytes 393224 | tf_op jit(solution)/shard_map/ppermute | solution.py:52
  39.9 6.0 %collective-permute-start.13 = (bf16[128,512]{1,0:T(8,128)(2,1)S(1)}, bf16[128,512]{1,0:T(8,128)(2,1)S(1)}, u32[]{:S(2)}, u32[]{:S(2)}) collective-permute-start(bf16[128,512]{1,0:T(8,128)(2,1)S(1)} %get-tuple-element.77.refs_7_), channel_id=1, source_target_pairs={{0,16},{16,0},{1,17},{17,1},{2,18},{18,2},{3,19},{19,3},{4,20},{20... | collective-permute-start | bytes 393224 | tf_op jit(solution)/shard_map/ppermute | solution.py:52
  46.8 1.7 %collective-permute-start.14 = (bf16[8,80,256]{2,1,0:T(8,128)(2,1)S(1)}, bf16[8,80,256]{2,1,0:T(8,128)(2,1)S(1)}, u32[]{:S(2)}, u32[]{:S(2)}) collective-permute-start(bf16[8,80,256]{2,1,0:T(8,128)(2,1)S(1)} %get-tuple-element.91), channel_id=1, source_target_pairs={{0,1},{1,0},{2,3},{3,2},{4,5},{5,4},{6,7},{7,6},{8,9},{9,8},{10,11... | collective-permute-start | bytes 983048 | tf_op jit(solution)/shard_map/ppermute | solution.py:56
  46.8 3.0 %collective-permute-start.17 = (bf16[8,80,256]{2,1,0:T(8,128)(2,1)S(1)}, bf16[8,80,256]{2,1,0:T(8,128)(2,1)S(1)}, u32[]{:S(2)}, u32[]{:S(2)}) collective-permute-start(bf16[8,80,256]{2,1,0:T(8,128)(2,1)S(1)} %get-tuple-element.93), channel_id=1, source_target_pairs={{0,1},{1,0},{2,3},{3,2},{4,5},{5,4},{6,7},{7,6},{8,9},{9,8},{10,11... | collective-permute-start | bytes 983048 | tf_op jit(solution)/shard_map/ppermute | solution.py:56
  48.5 5.4 %collective-permute-start.15 = (bf16[4,80,256]{2,1,0:T(8,128)(2,1)S(1)}, bf16[4,80,256]{2,1,0:T(8,128)(2,1)S(1)}, u32[]{:S(2)}, u32[]{:S(2)}) collective-permute-start(bf16[4,80,256]{2,1,0:T(8,128)(2,1)S(1)} %slice.91), channel_id=1, source_target_pairs={{0,2},{1,5},{2,0},{3,7},{4,6},{5,1},{6,4},{7,3},{8,10},{9,13},{10,... | collective-permute-start | bytes 491528 | tf_op jit(solution)/shard_map/ppermute | solution.py:48
  49.9 6.2 %collective-permute-start.18 = (bf16[4,80,256]{2,1,0:T(8,128)(2,1)S(1)}, bf16[4,80,256]{2,1,0:T(8,128)(2,1)S(1)}, u32[]{:S(2)}, u32[]{:S(2)}) collective-permute-start(bf16[4,80,256]{2,1,0:T(8,128)(2,1)S(1)} %slice.90), channel_id=1, source_target_pairs={{0,2},{1,5},{2,0},{3,7},{4,6},{5,1},{6,4},{7,3},{8,10},{9,13},{10,... | collective-permute-start | bytes 491528 | tf_op jit(solution)/shard_map/ppermute | solution.py:48
  54.0 4.5 %collective-permute-start.16 = (bf16[2,80,256]{2,1,0:T(8,128)(2,1)S(1)}, bf16[2,80,256]{2,1,0:T(8,128)(2,1)S(1)}, u32[]{:S(2)}, u32[]{:S(2)}) collective-permute-start(bf16[2,80,256]{2,1,0:T(8,128)(2,1)S(1)} %slice.93), channel_id=1, source_target_pairs={{0,4},{1,3},{2,6},{3,1},{4,0},{5,7},{6,2},{7,5},{8,12},{9,11},{10,... | collective-permute-start | bytes 245768 | tf_op jit(solution)/shard_map/ppermute | solution.py:48
  56.1 4.9 %collective-permute-start.19 = (bf16[2,80,256]{2,1,0:T(8,128)(2,1)S(1)}, bf16[2,80,256]{2,1,0:T(8,128)(2,1)S(1)}, u32[]{:S(2)}, u32[]{:S(2)}) collective-permute-start(bf16[2,80,256]{2,1,0:T(8,128)(2,1)S(1)} %slice.92), channel_id=1, source_target_pairs={{0,4},{1,3},{2,6},{3,1},{4,0},{5,7},{6,2},{7,5},{8,12},{9,11},{10,... | collective-permute-start | bytes 245768 | tf_op jit(solution)/shard_map/ppermute | solution.py:48
  58.5 7.8 %collective-permute-start.20 = (bf16[1,80,256]{2,1,0:T(8,128)(2,1)S(1)}, bf16[1,80,256]{2,1,0:T(8,128)(2,1)S(1)}, u32[]{:S(2)}, u32[]{:S(2)}) collective-permute-start(bf16[1,80,256]{2,1,0:T(8,128)(2,1)S(1)} %slice.95), channel_id=1, source_target_pairs={{0,8},{1,9},{2,10},{3,11},{4,12},{5,13},{6,14},{7,15},{8,0},{9,1},... | collective-permute-start | bytes 122888 | tf_op jit(solution)/shard_map/ppermute | solution.py:48
  61.1 5.2 %collective-permute-start.21 = (bf16[1,80,256]{2,1,0:T(8,128)(2,1)S(1)}, bf16[1,80,256]{2,1,0:T(8,128)(2,1)S(1)}, u32[]{:S(2)}, u32[]{:S(2)}) collective-permute-start(bf16[1,80,256]{2,1,0:T(8,128)(2,1)S(1)} %slice.94), channel_id=1, source_target_pairs={{0,8},{1,9},{2,10},{3,11},{4,12},{5,13},{6,14},{7,15},{8,0},{9,1},... | collective-permute-start | bytes 122888 | tf_op jit(solution)/shard_map/ppermute | solution.py:48
  (11 other events, 30.6 us)

commit v2 on v1

--- a/solution.py
+++ b/solution.py
@@ -321,11 +321,11 @@
             values[half + batch][...] = coord_grad[batch * count : (batch + 1) * count]
 
 
-def grads_kernel(*refs):
-    *inputs, kept_a, kept_b, sent_a, sent_b, hidden, gate_grad, next_grad, down_all, turned = refs
+def grads_kernel(theirs, *refs):
+    *inputs, block_a, block_b, hidden, gate_grad, next_grad, down_all, turned = refs
     turned0, hidden0, cotangent, *inputs = inputs
     batches, count, _ = cotangent.shape
-    places, _, width = kept_a.shape
+    places, _, width = block_a.shape
     section = lax.axis_index("section")
 
     @pl.when(section == 0)
@@ -353,12 +353,11 @@
     cuts = cuts_of(rows + extra * (down_all.shape[1] // width))
 
     def fill(source):
-        for index, target in enumerate(places_of(places, REDUCE[0])):
-            blocks = (kept_a, kept_b) if index < places else (sent_a, sent_b)
-            place = index % places
+        targets = places_of(places, REDUCE[0])
+        for place, target in enumerate(targets[places:] if theirs else targets[:places]):
             lines = down_all[pl.ds(pl.multiple_of(target * extra, extra), extra), :]
             gate = dot(source[pl.ds(pl.multiple_of(target * rows, rows), rows), :], gate_grad[...])
-            for cut, block in zip(cuts, blocks):
+            for cut, block in zip(cuts, (block_a, block_b)):
                 top = min(cut.stop, rows)
                 block[place, : top - cut.start, :] = gate[cut.start : top, :].astype(block.dtype)
                 if cut.stop > rows:
@@ -517,19 +516,25 @@
     )
     cuts = cuts_of(share_rows + down_rows * (coord_width // width))
     shapes = [(replicas // 2, cut.stop - cut.start, width) for cut in cuts]
-    blocks = call(
-        grads_kernel, [spec(shape, kind) for kind in (f32, bf16) for shape in shapes],
-        normed_turned, hidden, cotangent, *group0, *group1,
-        scratch=[
-            pltpu.VMEM((full, width), bf16), pltpu.VMEM((full, width), bf16),
-            pltpu.VMEM((full, coord_width), bf16), pltpu.VMEM((hidden_width, coord_width), f32),
-            pltpu.VMEM((model_width, full), bf16),
-        ],
-        flops=2 * full * width * (model_width + coord_width),
-        limit=16 << 20,
-    )
-    swapped = [swap_cores(sent, replicas) for sent in blocks[2:]]
-    totals = [kept + sent.astype(f32) for kept, sent in zip(blocks, swapped)]
+
+    def blocks_for(theirs):
+        return call(
+            functools.partial(grads_kernel, theirs), [spec(shape, bf16 if theirs else f32) for shape in shapes],
+            normed_turned, hidden, cotangent, *group0, *group1,
+            scratch=[
+                pltpu.VMEM((full, width), bf16), pltpu.VMEM((full, width), bf16),
+                pltpu.VMEM((full, coord_width), bf16), pltpu.VMEM((hidden_width, coord_width), f32),
+                pltpu.VMEM((model_width, full), bf16),
+            ],
+            flops=full * width * (model_width + coord_width),
+            limit=16 << 20,
+        )
+
+    swapped = []
+    for sent in blocks_for(True):
+        swapped.append(swap_cores(sent, replicas))
+    kept = blocks_for(False)
+    totals = [own + sent.astype(f32) for own, sent in zip(kept, swapped)]
     for turn in range(turns - 1, -1, -1):
         half = totals[0].shape[0] // 2
         come = []

time: 67.5 us -> 67.4 us (level)
    pallas_call x14 -> x15, Pallas kernels: 8.09 us -> 8.5 us  [call(): pl.pallas_call(body, out_shape=outs, in_specs=[pl.BlockSpec(memory_space=...]
  transfers between devices with their start and end apart: 22 -> 22, of which waited for: 9 -> 9; matrix products, arithmetic and copies ran while one was open for 1% -> 1% of each run, Pallas kernels for 8% -> 9%
where the time goes in v2:
time: 67.4 us; the launch traced here: 67.1 us
  starting transfers between devices  33.3 us (49%)
  waiting for transfers between devices  19 us (28%)
  Pallas kernels  8.5 us (13%)
  local copies, waits for them, and re-layouts  3.14 us (5%)
  other arithmetic  2.16 us (3%)
  between operations  0.99 us (1%)
    ppermute x12, starting transfers between devices, exchange(): return lax.ppermute(value, 'replica', pairs)  24.8 us
    ppermute x12, waiting for transfers between devices, exchange(): return lax.ppermute(value, 'replica', pairs)  12.6 us
    pallas_call x15, Pallas kernels, call(): pl.pallas_call(body, out_shape=outs, in_specs=[pl.BlockSpec(memory_space=...  8.5 us
    ppermute x4, starting transfers between devices, swap_sections(): return lax.ppermute(value, 'section', [(0, 1), (1, 0)])  7.4 us
    ppermute x4, waiting for transfers between devices, swap_sections(): return lax.ppermute(value, 'section', [(0, 1), (1, 0)])  5.86 us
    unnamed x26, local copies, waits for them, and re-layouts  3.05 us
  transfers between devices with their start and end apart: 22, of which 9 were waited for; matrix products, arithmetic and copies ran while one was open for 1% of the time, Pallas kernels for 9%

profile of v2, /device:TPU:0, one launch (start us, length us, event | category | flops | bytes accessed | tf_op | source)
XLA Modules:
  0.0 67.1 jit_solution(17016374580093406408)
XLA Ops:
  2.5 3.0 %collective-permute-start.4 = (bf16[1,160,256]{2,1,0:T(8,128)(2,1)S(1)}, bf16[1,160,256]{2,1,0:T(8,128)(2,1)S(1)}, u32[]{:S(2)}, u32[]{:S(2)}) collective-permute-start(bf16[1,160,256]{2,1,0:T(8,128)(2,1)S(1)} %maximum_bitcast_fusion), channel_id=1, source_target_pairs={{0,2},{1,9},{2,0},{3,11},{4,6},{5,13},{6,4},{7,15},{8,10},{9,1},{1... | collective-permute-start | bytes 245768 | tf_op jit(solution)/shard_map/ppermute | solution.py:48
  5.5 2.6 %collective-permute-start = (bf16[1,128,256]{2,1,0:T(8,128)(2,1)}, bf16[1,128,256]{2,1,0:T(8,128)(2,1)S(1)}, u32[]{:S(2)}, u32[]{:S(2)}) collective-permute-start(bf16[1,128,256]{2,1,0:T(8,128)(2,1)} %refs_0_.1), channel_id=1, source_target_pairs={{0,8},{1,9},{2,10},{3,11},{4,12},{5,13},{6,14},{7,15},{8,0},{9,1},... | collective-permute-start | bytes 196616 | tf_op jit(solution)/shard_map/ppermute | solution.py:48
  8.1 3.0 %collective-permute-start.5 = (bf16[2,160,256]{2,1,0:T(8,128)(2,1)S(1)}, bf16[2,160,256]{2,1,0:T(8,128)(2,1)S(1)}, u32[]{:S(2)}, u32[]{:S(2)}) collective-permute-start(bf16[2,160,256]{2,1,0:T(8,128)(2,1)S(1)} %pad_maximum_fusion.2), channel_id=1, source_target_pairs={{0,8},{1,5},{2,10},{3,7},{4,12},{5,1},{6,14},{7,3},{8,0},{9,13},{1... | collective-permute-start | bytes 491528 | tf_op jit(solution)/shard_map/ppermute | solution.py:48
  13.7 1.3 %collective-permute-done.5 = bf16[2,160,256]{2,1,0:T(8,128)(2,1)S(1)} collective-permute-done((bf16[2,160,256]{2,1,0:T(8,128)(2,1)S(1)}, bf16[2,160,256]{2,1,0:T(8,128)(2,1)S(1)}, u32[]{:S(2)}, u32[]{:S(2)}) %collective-permute-start.5) | collective-permute-done | bytes 163872 | tf_op jit(solution)/shard_map/ppermute | solution.py:48
  15.0 3.2 %collective-permute-start.6 = (bf16[4,160,256]{2,1,0:T(8,128)(2,1)S(1)}, bf16[4,160,256]{2,1,0:T(8,128)(2,1)S(1)}, u32[]{:S(2)}, u32[]{:S(2)}) collective-permute-start(bf16[4,160,256]{2,1,0:T(8,128)(2,1)S(1)} %pad_maximum_fusion.refs_1_), channel_id=1, source_target_pairs={{0,4},{1,3},{2,6},{3,1},{4,0},{5,7},{6,2},{7,5},{8,12},{9,11},{10,... | collective-permute-start | bytes 983048 | tf_op jit(solution)/shard_map/ppermute | solution.py:48
  18.2 1.1 %collective-permute-start.2 = (bf16[4,128,256]{2,1,0:T(8,128)(2,1)S(1)}, bf16[4,128,256]{2,1,0:T(8,128)(2,1)S(1)}, u32[]{:S(2)}, u32[]{:S(2)}) collective-permute-start(bf16[4,128,256]{2,1,0:T(8,128)(2,1)S(1)} %pad_maximum_fusion.1.refs_0_), channel_id=1, source_target_pairs={{0,2},{1,5},{2,0},{3,7},{4,6},{5,1},{6,4},{7,3},{8,10},{9,13},{10,... | collective-permute-start | bytes 786440 | tf_op jit(solution)/shard_map/ppermute | solution.py:48
  19.3 6.7 %collective-permute-done.6.refs_1_ = bf16[4,160,256]{2,1,0:T(8,128)(2,1)S(1)} collective-permute-done((bf16[4,160,256]{2,1,0:T(8,128)(2,1)S(1)}, bf16[4,160,256]{2,1,0:T(8,128)(2,1)S(1)}, u32[]{:S(2)}, u32[]{:S(2)}) %collective-permute-start.6) | collective-permute-done | bytes 327712 | tf_op jit(solution)/shard_map/ppermute | solution.py:48
  26.6 1.2 %copy-done.1 = bf16[2,128,2048]{2,1,0:T(8,128)(2,1)S(1)} copy-done((bf16[2,128,2048]{2,1,0:T(8,128)(2,1)S(1)}, bf16[2,128,2048]{2,1,0:T(8,128)(2,1)}, u32[]{:S(2)}) %copy-start.1) | copy-done | bytes 1048600
  27.8 0.9 %copy-done.4 = bf16[2,128,512]{2,1,0:T(8,128)(2,1)S(1)} copy-done((bf16[2,128,512]{2,1,0:T(8,128)(2,1)S(1)}, bf16[2,128,512]{2,1,0:T(8,128)(2,1)}, u32[]{:S(2)}) %copy-start.4) | copy-done | bytes 262168
  28.8 0.9 %shard_map.182 = (f32[256,2048]{1,0:T(8,128)S(1)}, bf16[256,2048]{1,0:T(8,128)(2,1)S(1)}, f32[256,128]{1,0:T(8,128)S(1)}) custom-call(bf16[256,512]{1,0:T(8,128)(2,1)S(1)} %bitcast.11, bf16[512,2048]{1,0:T(8,128)(2,1)S(1)} %copy-done, bf16[256,2048]{1,0:T(8,128)(2,1)S(1)} %bitcast.10, f32[1,2048]{1,0:T(1,128)S(1)} %copy-done.9), custom_call_target="tpu_custom_call" | custom-call | flops 536870912 | bytes 6692864 | tf_op jit(solution)/shard_map/pallas_call | solution.py:141
  29.9 0.9 %shard_map.183 = (bf16[2048,512]{1,0:T(8,128)(2,1)S(1)}, bf16[256,512]{1,0:T(8,128)(2,1)S(1)}, f32[256,512]{1,0:T(8,128)S(1)}, bf16[256,256]{1,0:T(8,128)(2,1)S(...) custom-call(bf16[4,128,256]{2,1,0:T(8,128)(2,1)S(1)} %collective-per, ...), custom_call_target="tpu_custom_call", output_to_operand_aliasing={{0}: (2, {}), {1}: (3, {})} | custom-call | flops 536870912 | bytes 7536640 | tf_op jit(solution)/shard_map/pallas_call | solution.py:141
  31.6 1.5 %shard_map.184 = (bf16[512,2048]{1,0:T(8,128)(2,1)S(1)}, bf16[512,256]{1,0:T(8,128)(2,1)S(1)}, bf16[2048,512]{1,0:T(8,128)(2,1)S(1)}, bf16[2048,256]{1,0:T(8,128)(2,1)S(1)}) custom-call(bf16[2048,512]{1,0:T(8,128)(2,1)S(1)} %get-tuple-element.61.refs_0_.refs_5_.refs_6_, bf16[256,512]{1,0:T(8,128)(2,1)S(1)} %get-tuple-element.62.refs_1_.refs_6_.refs_7_, ...), custom_call_target="tpu_custom_call" | custom-call | bytes 11010048 | tf_op jit(solution)/shard_map/pallas_call | solution.py:141
  33.1 1.4 %collective-permute-start.11 = (bf16[128,512]{1,0:T(8,128)(2,1)S(1)}, bf16[128,512]{1,0:T(8,128)(2,1)S(1)}, u32[]{:S(2)}, u32[]{:S(2)}) collective-permute-start(bf16[128,512]{1,0:T(8,128)(2,1)S(1)} %get-tuple-element.72.refs_1_), channel_id=1, source_target_pairs={{0,16},{16,0},{1,17},{17,1},{2,18},{18,2},{3,19},{19,3},{4,20},{20... | collective-permute-start | bytes 393224 | tf_op jit(solution)/shard_map/ppermute | solution.py:52
  34.5 2.8 %collective-permute-done.10.refs_0_ = bf16[128,512]{1,0:T(8,128)(2,1)S(1)} collective-permute-done((bf16[128,512]{1,0:T(8,128)(2,1)S(1)}, bf16[128,512]{1,0:T(8,128)(2,1)S(1)}, u32[]{:S(2)}, u32[]{:S(2)}) %collective-permute-start.10) | collective-permute-done | bytes 131104 | tf_op jit(solution)/shard_map/ppermute | solution.py:52
  37.3 2.6 %collective-permute-start.12 = (bf16[128,512]{1,0:T(8,128)(2,1)S(1)}, bf16[128,512]{1,0:T(8,128)(2,1)S(1)}, u32[]{:S(2)}, u32[]{:S(2)}) collective-permute-start(bf16[128,512]{1,0:T(8,128)(2,1)S(1)} %get-tuple-element.71.refs_0_.refs_6_), channel_id=1, source_target_pairs={{0,16},{16,0},{1,17},{17,1},{2,18},{18,2},{3,19},{19,3},{4,20},{20... | collective-permute-start | bytes 393224 | tf_op jit(solution)/shard_map/ppermute | solution.py:52
  39.9 2.7 %collective-permute-start.13 = (bf16[128,512]{1,0:T(8,128)(2,1)S(1)}, bf16[128,512]{1,0:T(8,128)(2,1)S(1)}, u32[]{:S(2)}, u32[]{:S(2)}) collective-permute-start(bf16[128,512]{1,0:T(8,128)(2,1)S(1)} %get-tuple-element.77.refs_7_), channel_id=1, source_target_pairs={{0,16},{16,0},{1,17},{17,1},{2,18},{18,2},{3,19},{19,3},{4,20},{20... | collective-permute-start | bytes 393224 | tf_op jit(solution)/shard_map/ppermute | solution.py:52
  43.4 2.5 %collective-permute-done.13.refs_8_.refs_1_.refs_5_ = bf16[128,512]{1,0:T(8,128)(2,1)S(1)} collective-permute-done((bf16[128,512]{1,0:T(8,128)(2,1)S(1)}, bf16[128,512]{1,0:T(8,128)(2,1)S(1)}, u32[]{:S(2)}, u32[]{:S(2)}) %collective-permute-start.13) | collective-permute-done | bytes 131104 | tf_op jit(solution)/shard_map/ppermute | solution.py:52
  48.4 1.3 %collective-permute-start.15 = (bf16[4,80,256]{2,1,0:T(8,128)(2,1)S(1)}, bf16[4,80,256]{2,1,0:T(8,128)(2,1)S(1)}, u32[]{:S(2)}, u32[]{:S(2)}) collective-permute-start(bf16[4,80,256]{2,1,0:T(8,128)(2,1)S(1)} %slice.91), channel_id=1, source_target_pairs={{0,2},{1,5},{2,0},{3,7},{4,6},{5,1},{6,4},{7,3},{8,10},{9,13},{10,... | collective-permute-start | bytes 491528 | tf_op jit(solution)/shard_map/ppermute | solution.py:48
  50.7 3.1 %collective-permute-done.15 = bf16[4,80,256]{2,1,0:T(8,128)(2,1)S(1)} collective-permute-done((bf16[4,80,256]{2,1,0:T(8,128)(2,1)S(1)}, bf16[4,80,256]{2,1,0:T(8,128)(2,1)S(1)}, u32[]{:S(2)}, u32[]{:S(2)}) %collective-permute-start.15) | collective-permute-done | bytes 163872 | tf_op jit(solution)/shard_map/ppermute | solution.py:48
  53.9 2.1 %collective-permute-start.16 = (bf16[2,80,256]{2,1,0:T(8,128)(2,1)S(1)}, bf16[2,80,256]{2,1,0:T(8,128)(2,1)S(1)}, u32[]{:S(2)}, u32[]{:S(2)}) collective-permute-start(bf16[2,80,256]{2,1,0:T(8,128)(2,1)S(1)} %slice.93), channel_id=1, source_target_pairs={{0,4},{1,3},{2,6},{3,1},{4,0},{5,7},{6,2},{7,5},{8,12},{9,11},{10,... | collective-permute-start | bytes 245768 | tf_op jit(solution)/shard_map/ppermute | solution.py:48
  56.0 1.7 %collective-permute-start.19 = (bf16[2,80,256]{2,1,0:T(8,128)(2,1)S(1)}, bf16[2,80,256]{2,1,0:T(8,128)(2,1)S(1)}, u32[]{:S(2)}, u32[]{:S(2)}) collective-permute-start(bf16[2,80,256]{2,1,0:T(8,128)(2,1)S(1)} %slice.92), channel_id=1, source_target_pairs={{0,4},{1,3},{2,6},{3,1},{4,0},{5,7},{6,2},{7,5},{8,12},{9,11},{10,... | collective-permute-start | bytes 245768 | tf_op jit(solution)/shard_map/ppermute | solution.py:48
  58.4 2.5 %collective-permute-start.20 = (bf16[1,80,256]{2,1,0:T(8,128)(2,1)S(1)}, bf16[1,80,256]{2,1,0:T(8,128)(2,1)S(1)}, u32[]{:S(2)}, u32[]{:S(2)}) collective-permute-start(bf16[1,80,256]{2,1,0:T(8,128)(2,1)S(1)} %slice.95), channel_id=1, source_target_pairs={{0,8},{1,9},{2,10},{3,11},{4,12},{5,13},{6,14},{7,15},{8,0},{9,1},... | collective-permute-start | bytes 122888 | tf_op jit(solution)/shard_map/ppermute | solution.py:48
  61.0 2.5 %collective-permute-start.21 = (bf16[1,80,256]{2,1,0:T(8,128)(2,1)S(1)}, bf16[1,80,256]{2,1,0:T(8,128)(2,1)S(1)}, u32[]{:S(2)}, u32[]{:S(2)}) collective-permute-start(bf16[1,80,256]{2,1,0:T(8,128)(2,1)S(1)} %slice.94), channel_id=1, source_target_pairs={{0,8},{1,9},{2,10},{3,11},{4,12},{5,13},{6,14},{7,15},{8,0},{9,1},... | collective-permute-start | bytes 122888 | tf_op jit(solution)/shard_map/ppermute | solution.py:48
  63.5 1.7 %shard_map.187 = (bf16[128,512]{1,0:T(8,128)(2,1)S(1)}, bf16[128,512]{1,0:T(8,128)(2,1)S(1)}) custom-call(f32[256,512]{1,0:T(8,128)S(1)} %get-tuple-element.74.refs_0_.refs_1_.refs_2_, f32[256,2048]{1,0:T(8,128)S(1)} %get-tuple-element.75.refs_1_, f32[256,128]{1,0:T(8,128)S(1)} %get-tuple-element.76.refs_2_, f32[1,2048]{1,0:T(1,128)S(1)} %copy-done.9, ...), custom_call_target="tpu_custom_call" | custom-call | flops 1073741824 | bytes 7741440 | tf_op jit(solution)/shard_map/pallas_call | solution.py:141
  (83 shorter events, 12.8 us)
Async XLA Ops:
  0.6 25.9 %copy-start.9 = (f32[1,2048]{1,0:T(1,128)S(1)}, f32[1,2048]{1,0:T(1,128)}, u32[]{:S(2)}) copy-start(f32[1,2048]{1,0:T(1,128)} %refs_3_.7) | copy-start | bytes 24580
  0.6 25.9 %copy-start = (bf16[512,2048]{1,0:T(8,128)(2,1)S(1)}, bf16[512,2048]{1,0:T(8,128)(2,1)}, u32[]{:S(2)}) copy-start(bf16[512,2048]{1,0:T(8,128)(2,1)} %refs_3_.6) | copy-start | bytes 6291460
  2.5 5.6 %collective-permute-start.4 = (bf16[1,160,256]{2,1,0:T(8,128)(2,1)S(1)}, bf16[1,160,256]{2,1,0:T(8,128)(2,1)S(1)}, u32[]{:S(2)}, u32[]{:S(2)}) collective-permute-start(bf16[1,160,256]{2,1,0:T(8,128)(2,1)S(1)} %maximum_bitcast_fusion), channel_id=1, source_target_pairs={{0,2},{1,9},{2,0},{3,11},{4,6},{5,13},{6,4},{7,15},{8,10},{9,1},{1... | collective-permute-start | bytes 245768 | tf_op jit(solution)/shard_map/ppermute | solution.py:48
  5.5 7.3 %collective-permute-start = (bf16[1,128,256]{2,1,0:T(8,128)(2,1)}, bf16[1,128,256]{2,1,0:T(8,128)(2,1)S(1)}, u32[]{:S(2)}, u32[]{:S(2)}) collective-permute-start(bf16[1,128,256]{2,1,0:T(8,128)(2,1)} %refs_0_.1), channel_id=1, source_target_pairs={{0,8},{1,9},{2,10},{3,11},{4,12},{5,13},{6,14},{7,15},{8,0},{9,1},... | collective-permute-start | bytes 196616 | tf_op jit(solution)/shard_map/ppermute | solution.py:48
  8.1 6.8 %collective-permute-start.5 = (bf16[2,160,256]{2,1,0:T(8,128)(2,1)S(1)}, bf16[2,160,256]{2,1,0:T(8,128)(2,1)S(1)}, u32[]{:S(2)}, u32[]{:S(2)}) collective-permute-start(bf16[2,160,256]{2,1,0:T(8,128)(2,1)S(1)} %pad_maximum_fusion.2), channel_id=1, source_target_pairs={{0,8},{1,5},{2,10},{3,7},{4,12},{5,1},{6,14},{7,3},{8,0},{9,13},{1... | collective-permute-start | bytes 491528 | tf_op jit(solution)/shard_map/ppermute | solution.py:48
  12.8 5.4 %collective-permute-start.1 = (bf16[2,128,256]{2,1,0:T(8,128)(2,1)S(1)}, bf16[2,128,256]{2,1,0:T(8,128)(2,1)S(1)}, u32[]{:S(2)}, u32[]{:S(2)}) collective-permute-start(bf16[2,128,256]{2,1,0:T(8,128)(2,1)S(1)} %pad_maximum_fusion.3), channel_id=1, source_target_pairs={{0,4},{1,3},{2,6},{3,1},{4,0},{5,7},{6,2},{7,5},{8,12},{9,11},{10,... | collective-permute-start | bytes 393224 | tf_op jit(solution)/shard_map/ppermute | solution.py:48
  15.0 11.0 %collective-permute-start.6 = (bf16[4,160,256]{2,1,0:T(8,128)(2,1)S(1)}, bf16[4,160,256]{2,1,0:T(8,128)(2,1)S(1)}, u32[]{:S(2)}, u32[]{:S(2)}) collective-permute-start(bf16[4,160,256]{2,1,0:T(8,128)(2,1)S(1)} %pad_maximum_fusion.refs_1_), channel_id=1, source_target_pairs={{0,4},{1,3},{2,6},{3,1},{4,0},{5,7},{6,2},{7,5},{8,12},{9,11},{10,... | collective-permute-start | bytes 983048 | tf_op jit(solution)/shard_map/ppermute | solution.py:48
  18.2 8.3 %collective-permute-start.2 = (bf16[4,128,256]{2,1,0:T(8,128)(2,1)S(1)}, bf16[4,128,256]{2,1,0:T(8,128)(2,1)S(1)}, u32[]{:S(2)}, u32[]{:S(2)}) collective-permute-start(bf16[4,128,256]{2,1,0:T(8,128)(2,1)S(1)} %pad_maximum_fusion.1.refs_0_), channel_id=1, source_target_pairs={{0,2},{1,5},{2,0},{3,7},{4,6},{5,1},{6,4},{7,3},{8,10},{9,13},{10,... | collective-permute-start | bytes 786440 | tf_op jit(solution)/shard_map/ppermute | solution.py:48
  19.3 10.4 %collective-permute-start.9 = (bf16[4,160,256]{2,1,0:T(8,128)(2,1)S(1)}, bf16[4,160,256]{2,1,0:T(8,128)(2,1)S(1)}, u32[]{:S(2)}, u32[]{:S(2)}) collective-permute-start(bf16[4,160,256]{2,1,0:T(8,128)(2,1)S(1)} %pad_maximum_fusion.refs_1_), channel_id=1, source_target_pairs={{0,1},{1,0},{2,3},{3,2},{4,5},{5,4},{6,7},{7,6},{8,9},{9,8},{10,11... | collective-permute-start | bytes 983048 | tf_op jit(solution)/shard_map/ppermute | solution.py:56
  26.0 3.9 %collective-permute-start.7 = (bf16[4,160,256]{2,1,0:T(8,128)(2,1)S(1)}, bf16[4,160,256]{2,1,0:T(8,128)(2,1)S(1)}, u32[]{:S(2)}, u32[]{:S(2)}) collective-permute-start(bf16[4,160,256]{2,1,0:T(8,128)(2,1)S(1)} %collective-permute-done.6.refs_1_), channel_id=1, source_target_pairs={{0,1},{1,0},{2,3},{3,2},{4,5},{5,4},{6,7},{7,6},{8,9},{9,8},{10,11... | collective-permute-start | bytes 983048 | tf_op jit(solution)/shard_map/ppermute | solution.py:56
  26.1 3.6 %collective-permute-start.8 = (bf16[4,128,256]{2,1,0:T(8,128)(2,1)S(1)}, bf16[4,128,256]{2,1,0:T(8,128)(2,1)S(1)}, u32[]{:S(2)}, u32[]{:S(2)}) collective-permute-start(bf16[4,128,256]{2,1,0:T(8,128)(2,1)S(1)} %pad_maximum_fusion.1.refs_0_), channel_id=1, source_target_pairs={{0,1},{1,0},{2,3},{3,2},{4,5},{5,4},{6,7},{7,6},{8,9},{9,8},{10,11... | collective-permute-start | bytes 786440 | tf_op jit(solution)/shard_map/ppermute | solution.py:56
  26.6 3.3 %collective-permute-start.3 = (bf16[4,128,256]{2,1,0:T(8,128)(2,1)S(1)}, bf16[4,128,256]{2,1,0:T(8,128)(2,1)S(1)}, u32[]{:S(2)}, u32[]{:S(2)}) collective-permute-start(bf16[4,128,256]{2,1,0:T(8,128)(2,1)S(1)} %collective-permute-done.2.refs_0_), channel_id=1, source_target_pairs={{0,1},{1,0},{2,3},{3,2},{4,5},{5,4},{6,7},{7,6},{8,9},{9,8},{10,11... | collective-permute-start | bytes 786440 | tf_op jit(solution)/shard_map/ppermute | solution.py:56
  30.8 6.4 %collective-permute-start.10 = (bf16[128,512]{1,0:T(8,128)(2,1)S(1)}, bf16[128,512]{1,0:T(8,128)(2,1)S(1)}, u32[]{:S(2)}, u32[]{:S(2)}) collective-permute-start(bf16[128,512]{1,0:T(8,128)(2,1)S(1)} %get-tuple-element.59.refs_0_), channel_id=1, source_target_pairs={{0,16},{16,0},{1,17},{17,1},{2,18},{18,2},{3,19},{19,3},{4,20},{20... | collective-permute-start | bytes 393224 | tf_op jit(solution)/shard_map/ppermute | solution.py:52
  33.1 6.8 %collective-permute-start.11 = (bf16[128,512]{1,0:T(8,128)(2,1)S(1)}, bf16[128,512]{1,0:T(8,128)(2,1)S(1)}, u32[]{:S(2)}, u32[]{:S(2)}) collective-permute-start(bf16[128,512]{1,0:T(8,128)(2,1)S(1)} %get-tuple-element.72.refs_1_), channel_id=1, source_target_pairs={{0,16},{16,0},{1,17},{17,1},{2,18},{18,2},{3,19},{19,3},{4,20},{20... | collective-permute-start | bytes 393224 | tf_op jit(solution)/shard_map/ppermute | solution.py:52
  37.3 5.9 %collective-permute-start.12 = (bf16[128,512]{1,0:T(8,128)(2,1)S(1)}, bf16[128,512]{1,0:T(8,128)(2,1)S(1)}, u32[]{:S(2)}, u32[]{:S(2)}) collective-permute-start(bf16[128,512]{1,0:T(8,128)(2,1)S(1)} %get-tuple-element.71.refs_0_.refs_6_), channel_id=1, source_target_pairs={{0,16},{16,0},{1,17},{17,1},{2,18},{18,2},{3,19},{19,3},{4,20},{20... | collective-permute-start | bytes 393224 | tf_op jit(solution)/shard_map/ppermute | solution.py:52
  39.9 6.0 %collective-permute-start.13 = (bf16[128,512]{1,0:T(8,128)(2,1)S(1)}, bf16[128,512]{1,0:T(8,128)(2,1)S(1)}, u32[]{:S(2)}, u32[]{:S(2)}) collective-permute-start(bf16[128,512]{1,0:T(8,128)(2,1)S(1)} %get-tuple-element.77.refs_7_), channel_id=1, source_target_pairs={{0,16},{16,0},{1,17},{17,1},{2,18},{18,2},{3,19},{19,3},{4,20},{20... | collective-permute-start | bytes 393224 | tf_op jit(solution)/shard_map/ppermute | solution.py:52
  46.6 1.7 %collective-permute-start.14 = (bf16[8,80,256]{2,1,0:T(8,128)(2,1)S(1)}, bf16[8,80,256]{2,1,0:T(8,128)(2,1)S(1)}, u32[]{:S(2)}, u32[]{:S(2)}) collective-permute-start(bf16[8,80,256]{2,1,0:T(8,128)(2,1)S(1)} %get-tuple-element.91), channel_id=1, source_target_pairs={{0,1},{1,0},{2,3},{3,2},{4,5},{5,4},{6,7},{7,6},{8,9},{9,8},{10,11... | collective-permute-start | bytes 983048 | tf_op jit(solution)/shard_map/ppermute | solution.py:56
  46.7 3.0 %collective-permute-start.17 = (bf16[8,80,256]{2,1,0:T(8,128)(2,1)S(1)}, bf16[8,80,256]{2,1,0:T(8,128)(2,1)S(1)}, u32[]{:S(2)}, u32[]{:S(2)}) collective-permute-start(bf16[8,80,256]{2,1,0:T(8,128)(2,1)S(1)} %get-tuple-element.93), channel_id=1, source_target_pairs={{0,1},{1,0},{2,3},{3,2},{4,5},{5,4},{6,7},{7,6},{8,9},{9,8},{10,11... | collective-permute-start | bytes 983048 | tf_op jit(solution)/shard_map/ppermute | solution.py:56
  48.4 5.4 %collective-permute-start.15 = (bf16[4,80,256]{2,1,0:T(8,128)(2,1)S(1)}, bf16[4,80,256]{2,1,0:T(8,128)(2,1)S(1)}, u32[]{:S(2)}, u32[]{:S(2)}) collective-permute-start(bf16[4,80,256]{2,1,0:T(8,128)(2,1)S(1)} %slice.91), channel_id=1, source_target_pairs={{0,2},{1,5},{2,0},{3,7},{4,6},{5,1},{6,4},{7,3},{8,10},{9,13},{10,... | collective-permute-start | bytes 491528 | tf_op jit(solution)/shard_map/ppermute | solution.py:48
  49.8 6.2 %collective-permute-start.18 = (bf16[4,80,256]{2,1,0:T(8,128)(2,1)S(1)}, bf16[4,80,256]{2,1,0:T(8,128)(2,1)S(1)}, u32[]{:S(2)}, u32[]{:S(2)}) collective-permute-start(bf16[4,80,256]{2,1,0:T(8,128)(2,1)S(1)} %slice.90), channel_id=1, source_target_pairs={{0,2},{1,5},{2,0},{3,7},{4,6},{5,1},{6,4},{7,3},{8,10},{9,13},{10,... | collective-permute-start | bytes 491528 | tf_op jit(solution)/shard_map/ppermute | solution.py:48
  53.9 4.5 %collective-permute-start.16 = (bf16[2,80,256]{2,1,0:T(8,128)(2,1)S(1)}, bf16[2,80,256]{2,1,0:T(8,128)(2,1)S(1)}, u32[]{:S(2)}, u32[]{:S(2)}) collective-permute-start(bf16[2,80,256]{2,1,0:T(8,128)(2,1)S(1)} %slice.93), channel_id=1, source_target_pairs={{0,4},{1,3},{2,6},{3,1},{4,0},{5,7},{6,2},{7,5},{8,12},{9,11},{10,... | collective-permute-start | bytes 245768 | tf_op jit(solution)/shard_map/ppermute | solution.py:48
  56.0 4.9 %collective-permute-start.19 = (bf16[2,80,256]{2,1,0:T(8,128)(2,1)S(1)}, bf16[2,80,256]{2,1,0:T(8,128)(2,1)S(1)}, u32[]{:S(2)}, u32[]{:S(2)}) collective-permute-start(bf16[2,80,256]{2,1,0:T(8,128)(2,1)S(1)} %slice.92), channel_id=1, source_target_pairs={{0,4},{1,3},{2,6},{3,1},{4,0},{5,7},{6,2},{7,5},{8,12},{9,11},{10,... | collective-permute-start | bytes 245768 | tf_op jit(solution)/shard_map/ppermute | solution.py:48
  58.4 7.8 %collective-permute-start.20 = (bf16[1,80,256]{2,1,0:T(8,128)(2,1)S(1)}, bf16[1,80,256]{2,1,0:T(8,128)(2,1)S(1)}, u32[]{:S(2)}, u32[]{:S(2)}) collective-permute-start(bf16[1,80,256]{2,1,0:T(8,128)(2,1)S(1)} %slice.95), channel_id=1, source_target_pairs={{0,8},{1,9},{2,10},{3,11},{4,12},{5,13},{6,14},{7,15},{8,0},{9,1},... | collective-permute-start | bytes 122888 | tf_op jit(solution)/shard_map/ppermute | solution.py:48
  61.0 5.2 %collective-permute-start.21 = (bf16[1,80,256]{2,1,0:T(8,128)(2,1)S(1)}, bf16[1,80,256]{2,1,0:T(8,128)(2,1)S(1)}, u32[]{:S(2)}, u32[]{:S(2)}) collective-permute-start(bf16[1,80,256]{2,1,0:T(8,128)(2,1)S(1)} %slice.94), channel_id=1, source_target_pairs={{0,8},{1,9},{2,10},{3,11},{4,12},{5,13},{6,14},{7,15},{8,0},{9,1},... | collective-permute-start | bytes 122888 | tf_op jit(solution)/shard_map/ppermute | solution.py:48
  (11 other events, 30.6 us)
